TPU v7x, 512 devices: a whole 4x8x8 slice. The times are simulated.
512 devices in a mesh: exp: 16 (over y, core), space: 32 (over z, x).
Axes of the slice: x: 4, y: 8, z: 8, core: 2. Of those that a mesh axis runs over, the one named last changes fastest.
Arguments:
- initial: float32 [16, 4, 64, 64, 128], P('exp', None, 'space'), may hold values from -6 to 6
- cotangent: float32 [16, 4, 64, 64, 128], P('exp', None, 'space'), may hold values from -6 to 6
- permeability: float32 [64, 64, 128], P('space'), may hold values from 0.25 to 1.25
- labels: int32 [64, 64, 128], P('space'), may hold values from 0 to 511
- comp_scale: float32 [4], replicated, may hold values from 0.3 to 1
- coupling_mask: int32 [4, 4], replicated, may hold values from 0 to 1
- coupling_rate: float32 [4, 4], replicated, may hold values from 0.05 to 0.5
- dose: float32 [16], P('exp'), may hold values from 50 to 200
- inject_voxel: int32 [16], P('exp'), may hold values from 0 to 524287
- arrival: int32 [16], P('exp'), may hold values from 0 to 4
Outputs:
- concentration: float32 [16, 4, 64, 64, 128], P('exp', None, 'space')
- sensitivity: float32 [16, 4, 64, 64, 128], P('exp', None, 'space')
- perm_gradient: float32 [512], replicated
All inputs are finite; a program needn't handle non-finite values.
Results may differ from a plain program's by a relative error of at most 0.0003.
Values sent between devices are 32-bit elements; how exact they have to be, the bound alone decides.
No kernel may reach another device: no remote copies, remote signals or barrier semaphores. Data moves between devices by JAX's collectives and lax.ppermute only.
A program may use at most 64 MiB of HBM per device.

v0:
```python
import math

import jax
import jax.numpy as jnp
from jax import lax
from jax.sharding import PartitionSpec as P

STEPS = 5
LABELS = 512


time_step = 0.1


def extended(block, sides, width):
    for axis, dim in sides:
        count = lax.axis_size(axis)
        forward = [(i, i + 1) for i in range(count - 1)]
        backward = [(target, source) for source, target in forward]
        low = lax.ppermute(
            lax.slice_in_dim(block, block.shape[dim] - width, None, axis=dim), axis, forward
        )
        high = lax.ppermute(lax.slice_in_dim(block, 0, width, axis=dim), axis, backward)
        block = jnp.concatenate([low, block, high], axis=dim)
    return block


def sides(padded):
    return [
        padded[..., 2:, 1:-1, 1:-1],
        padded[..., :-2, 1:-1, 1:-1],
        padded[..., 1:-1, 2:, 1:-1],
        padded[..., 1:-1, :-2, 1:-1],
        padded[..., 1:-1, 1:-1, 2:],
        padded[..., 1:-1, 1:-1, :-2],
    ]


def widen(field):
    return jnp.pad(field, ((0, 0), (0, 0), (1, 1), (1, 1)))


def coupling(coupling_mask, coupling_rate):
    size = coupling_rate.shape[0]
    off = (
        coupling_mask.astype(jnp.float32) * coupling_rate * (1.0 - jnp.eye(size, dtype=jnp.float32))
    )
    return off - jnp.diag(jnp.sum(off, axis=1))


def on_device(
    initial,
    cotangent,
    permeability,
    labels,
    comp_scale,
    coupling_mask,
    coupling_rate,
    dose,
    inject_voxel,
    arrival,
):
    rows, wide, deep = permeability.shape
    perm_pad = extended(permeability, (("space", 0),), 1)
    perm_pad = jnp.pad(perm_pad, ((0, 0), (1, 1), (1, 1)))
    faces = [0.5 * (permeability + near) for near in sides(perm_pad)]
    mixing = coupling(coupling_mask, coupling_rate)
    scale = comp_scale[:, None, None, None]

    def laplace(padded, center):
        total = jnp.zeros_like(center)
        for coef, near in zip(faces, sides(padded)):
            total = total + coef * (near - center)
        return total

    offset = lax.axis_index("space") * rows
    plane_x = offset + lax.broadcasted_iota(jnp.int32, (rows, wide, deep), 0)
    plane_y = lax.broadcasted_iota(jnp.int32, (rows, wide, deep), 1)
    plane_z = lax.broadcasted_iota(jnp.int32, (rows, wide, deep), 2)
    flat = (plane_x * wide + plane_y) * deep + plane_z
    spot = (flat == inject_voxel[0]).astype(jnp.float32)
    state = initial[0]
    stored = []
    for step in range(STEPS):
        padded = widen(extended(state, (("space", 1),), 1))
        stored.append(padded)
        flow = scale * laplace(padded, state)
        flow = flow + jnp.einsum("cd,dxyz->cxyz", mixing, state, precision=lax.Precision.HIGHEST)
        pulse = jnp.where(step >= arrival[0], dose[0], 0.0) * time_step * spot
        state = state + time_step * flow
        state = state.at[0].add(pulse)
    adjoint = cotangent[0]
    grad = jnp.zeros((rows, wide, deep), jnp.float32)
    for step in reversed(range(STEPS)):
        padded_u = stored[step]
        padded_l = widen(extended(adjoint, (("space", 1),), 1))
        center_u = padded_u[:, 1:-1, 1:-1, 1:-1]
        product = jnp.zeros_like(adjoint)
        for near_l, near_u in zip(sides(padded_l), sides(padded_u)):
            product = product + (near_l - adjoint) * (near_u - center_u)
        grad = grad + jnp.sum(scale * product, axis=0)
        flow = scale * laplace(padded_l, adjoint)
        flow = flow + jnp.einsum("dc,dxyz->cxyz", mixing, adjoint, precision=lax.Precision.HIGHEST)
        adjoint = adjoint + time_step * flow
    weighted = -0.5 * time_step * grad * permeability
    flat_labels = labels.reshape(-1)
    summed = lax.psum(weighted, "exp")
    binned = jax.ops.segment_sum(summed.reshape(-1), flat_labels, num_segments=LABELS)
    total = lax.psum(binned, "space")
    norm_factor = math.sqrt(
        rows * lax.axis_size("space") * wide * deep * lax.axis_size("exp") / LABELS
    )
    return (state[None], adjoint[None], total / norm_factor)


def solution(mesh):
    return jax.shard_map(
        on_device,
        mesh=mesh,
        in_specs=(
            P("exp", None, "space", None, None),
            P("exp", None, "space", None, None),
            P("space", None, None),
            P("space", None, None),
            P(),
            P(),
            P(),
            P("exp"),
            P("exp"),
            P("exp"),
        ),
        out_specs=(P("exp", None, "space", None, None), P("exp", None, "space", None, None), P()),
        check_vma=False,
    )
```

profile of v0, /device:TPU:8, one launch (start us, length us, event | category | flops | bytes accessed | tf_op | source)
XLA Modules:
  0.0 471.1 jit_solution(2731218075138146100)
XLA Ops:
  7.2 0.8 fusion.79
  8.0 3.5 collective-permute-start.2
  11.6 1.4 collective-permute-start
  13.0 1.1 copy.36
  14.2 4.6 collective-permute-start.13
  18.8 1.3 collective-permute-start.12
  20.3 4.6 collective-permute-start.3
  27.0 1.3 collective-permute-start.1
  28.7 5.2 %collective-permute-done.1 = f32[4,1,64,128]{3,0,2,1:T(4,128)S(1)} collective-permute-done((f32[4,1,64,128]{3,0,2,1:T(4,128)S(1)}, f32[4,1,64,128]{3,0,2,1:T(4,128)S(1)}, u32[]{:S(2)}, u32[]{:S(2)}) %collective-permute-start.1) | collective-permute-done | bytes 131104 | tf_op jit(solution)/shard_map/ppermute | solution.py:23
  34.5 0.8 fusion.20
  35.5 1.3 scatter-add.24
  36.9 5.0 %collective-permute-start.5 = (f32[4,1,64,128]{3,0,2,1:T(4,128)S(1)}, f32[4,1,64,128]{3,0,2,1:T(4,128)S(1)}, u32[]{:S(2)}, u32[]{:S(2)}) collective-permute-start(f32[4,1,64,128]{3,0,2,1:T(4,128)S(1)} %get-tuple-element.86), channel_id=1, source_target_pairs={{0,1},{1,2},{2,3},{3,4},{4,5},{5,6},{6,7},{7,8},{8,9},{9,10},{10,1... | collective-permute-start | bytes 393224 | tf_op jit(solution)/shard_map/ppermute | solution.py:20
  41.9 1.3 collective-permute-start.4
  43.9 1.1 fusion.10
  45.1 0.7 fusion.72
  45.8 7.3 %collective-permute-start.15 = (f32[4,1,64,128]{3,0,2,1:T(4,128)}, f32[4,1,64,128]{3,0,2,1:T(4,128)}, u32[]{:S(2)}, u32[]{:S(2)}) collective-permute-start(f32[4,1,64,128]{3,0,2,1:T(4,128)} %get-tuple-element.76), channel_id=1, source_target_pairs={{0,1},{1,2},{2,3},{3,4},{4,5},{5,6},{6,7},{7,8},{8,9},{9,10},{10,1... | collective-permute-start | bytes 393224 | tf_op jit(solution)/shard_map/ppermute | solution.py:20
  53.1 1.3 collective-permute-start.14
  55.2 1.0 fusion.18
  56.9 0.8 slice_add_fusion.3
  57.7 2.8 scatter-add.25
  60.5 1.0 fusion.76
  61.5 6.0 %collective-permute-start.7 = (f32[4,1,64,128]{3,0,2,1:T(4,128)S(1)}, f32[4,1,64,128]{3,0,2,1:T(4,128)S(1)}, u32[]{:S(2)}, u32[]{:S(2)}) collective-permute-start(f32[4,1,64,128]{3,0,2,1:T(4,128)S(1)} %get-tuple-element.84), channel_id=1, source_target_pairs={{0,1},{1,2},{2,3},{3,4},{4,5},{5,6},{6,7},{7,8},{8,9},{9,10},{10,1... | collective-permute-start | bytes 393224 | tf_op jit(solution)/shard_map/ppermute | solution.py:20
  67.6 1.3 collective-permute-start.6
  68.9 1.7 select_maximum_fusion.6
  70.6 2.6 fusion.8
  73.2 0.8 fusion.71
  74.0 5.2 %collective-permute-start.17 = (f32[4,1,64,128]{3,0,2,1:T(4,128)}, f32[4,1,64,128]{3,0,2,1:T(4,128)}, u32[]{:S(2)}, u32[]{:S(2)}) collective-permute-start(f32[4,1,64,128]{3,0,2,1:T(4,128)} %get-tuple-element.74), channel_id=1, source_target_pairs={{0,1},{1,2},{2,3},{3,4},{4,5},{5,6},{6,7},{7,8},{8,9},{9,10},{10,1... | collective-permute-start | bytes 393224 | tf_op jit(solution)/shard_map/ppermute | solution.py:20
  79.2 1.5 collective-permute-start.16
  81.3 1.0 fusion.16
  82.4 0.7 copy-done.14
  83.1 0.8 slice_add_fusion.2
  83.9 2.8 scatter-add.26
  86.7 1.0 fusion.75
  87.7 4.6 collective-permute-start.9
  92.3 1.3 collective-permute-start.8
  93.6 1.7 select_maximum_fusion.4
  95.4 2.3 fusion.6
  97.7 0.8 fusion.70
  98.4 6.8 %collective-permute-start.19 = (f32[4,1,64,128]{3,0,2,1:T(4,128)}, f32[4,1,64,128]{3,0,2,1:T(4,128)}, u32[]{:S(2)}, u32[]{:S(2)}) collective-permute-start(f32[4,1,64,128]{3,0,2,1:T(4,128)} %get-tuple-element.72), channel_id=1, source_target_pairs={{0,1},{1,2},{2,3},{3,4},{4,5},{5,6},{6,7},{7,8},{8,9},{9,10},{10,1... | collective-permute-start | bytes 393224 | tf_op jit(solution)/shard_map/ppermute | solution.py:20
  105.2 1.4 collective-permute-start.18
  106.7 2.5 multiply_reduce_fusion.2
  109.8 1.0 fusion.14
  111.5 0.8 slice_add_fusion.1
  112.3 2.8 scatter-add.29
  115.2 1.0 fusion.74
  116.2 6.0 %collective-permute-start.11 = (f32[4,1,64,128]{3,0,2,1:T(4,128)S(1)}, f32[4,1,64,128]{3,0,2,1:T(4,128)S(1)}, u32[]{:S(2)}, u32[]{:S(2)}) collective-permute-start(f32[4,1,64,128]{3,0,2,1:T(4,128)S(1)} %get-tuple-element.80), channel_id=1, source_target_pairs={{0,1},{1,2},{2,3},{3,4},{4,5},{5,6},{6,7},{7,8},{8,9},{9,10},{10,1... | collective-permute-start | bytes 393224 | tf_op jit(solution)/shard_map/ppermute | solution.py:20
  122.3 1.3 collective-permute-start.10
  123.6 1.7 select_maximum_fusion.2
  125.4 2.3 fusion.4
  127.7 6.7 %collective-permute-start.21 = (f32[4,1,64,128]{3,0,2,1:T(4,128)S(1)}, f32[4,1,64,128]{3,0,2,1:T(4,128)S(1)}, u32[]{:S(2)}, u32[]{:S(2)}) collective-permute-start(f32[4,1,64,128]{3,0,2,1:T(4,128)S(1)} %get-tuple-element.70), channel_id=1, source_target_pairs={{0,1},{1,2},{2,3},{3,4},{4,5},{5,6},{6,7},{7,8},{8,9},{9,10},{10,1... | collective-permute-start | bytes 393224 | tf_op jit(solution)/shard_map/ppermute | solution.py:20
  134.4 1.6 collective-permute-start.20
  136.1 1.9 multiply_reduce_fusion.3
  138.0 1.9 multiply_reduce_fusion.1
  141.1 0.9 multiply_reduce_fusion.4
  142.1 1.4 collective-permute-done.20
  144.2 0.9 multiply_reduce_fusion
  145.9 2.2 fusion.12
  148.2 1.1 fusion.2
  149.5 1.3 scatter-add.36
  150.8 0.7 copy.21
  151.6 0.7 copy.22
  152.3 122.5 %all-reduce.13.cloned.1.call-done = f32[16384]{0:T(1024)} async-done(((f32[16384]{0:T(1024)}), f32[16384]{0:T(1024)}) %all-reduce.13.cloned.1.call-update) | async-done | bytes 65552 | tf_op jit(solution)/shard_map/psum | solution.py:107
  274.8 113.6 %scatter_custom_fusion = f32[512]{0:T(512)S(1)} fusion(s32[16384]{0:T(1024)} %bitcast.74, f32[16384]{0:T(1024)} %all-reduce.13.cloned.1.call-done, f32[]{:T(128)} %constant.150.clone.1), kind=kCustom, calls=%fused_computation.191 | custom fusion | flops 16384 | bytes 2560 | tf_op jit(solution)/shard_map/scatter-add | solution.py:108
  388.3 75.4 %psum.15 = f32[512]{0:T(512)S(1)} all-reduce(f32[512]{0:T(512)S(1)} %scatter_custom_fusion), channel_id=1, replica_groups=mesh['exp'=16,'space'=32] {'space'}, use_global_device_ids=true, to_apply=%region_8.9 | all-reduce | flops 512 | bytes 4096 | tf_op jit(solution)/shard_map/psum | solution.py:109
  (236 shorter events, 8.9 us)
Async XLA Ops:
  7.2 12.9 %copy-start.57 = (f32[1,4,2,64,128]{4,3,2,1,0:T(8,128)S(1)}, f32[1,4,2,64,128]{4,3,2,1,0:T(8,128)}, u32[]{:S(2)}) copy-start(f32[1,4,2,64,128]{4,3,2,1,0:T(8,128)} %param.20) | copy-start | bytes 786436
  7.2 267.6 %all-reduce.13.cloned.1.call-start = ((), (), s32[]{:S(2)}) async-start(), calls=%async_computation | async-start | bytes 131072 | tf_op jit(solution)/shard_map/psum | solution.py:107
  8.0 16.8 %copy-start.95 = (f32[4,4]{1,0:T(4,128)S(1)}, f32[4,4]{1,0:T(4,128)}, u32[]{:S(2)}) copy-start(f32[4,4]{1,0:T(4,128)} %param.26) | copy-start | bytes 196
  8.0 16.8 %copy-start.96 = (s32[4,4]{1,0:T(4,128)S(1)}, s32[4,4]{1,0:T(4,128)}, u32[]{:S(2)}) copy-start(s32[4,4]{1,0:T(4,128)} %param.25) | copy-start | bytes 196
  8.0 19.0 %collective-permute-start.2 = (f32[1,64,128]{2,1,0:T(8,128)S(1)}, f32[1,64,128]{2,1,0:T(8,128)S(1)}, u32[]{:S(2)}, u32[]{:S(2)}) collective-permute-start(f32[1,64,128]{2,1,0:T(8,128)S(1)} %get-tuple-element.92), channel_id=1, source_target_pairs={{0,1},{1,2},{2,3},{3,4},{4,5},{5,6},{6,7},{7,8},{8,9},{9,10},{10,1... | collective-permute-start | bytes 98312 | tf_op jit(solution)/shard_map/ppermute | solution.py:20
  11.6 16.8 %copy-start.28 = (f32[2,64,128]{2,1,0:T(8,128)S(1)}, f32[2,64,128]{2,1,0:T(8,128)}, u32[]{:S(2)}) copy-start(f32[2,64,128]{2,1,0:T(8,128)} %param.22) | copy-start | bytes 196612
  11.6 16.7 %collective-permute-start = (f32[1,64,128]{2,1,0:T(8,128)S(1)}, f32[1,64,128]{2,1,0:T(8,128)S(1)}, u32[]{:S(2)}, u32[]{:S(2)}) collective-permute-start(f32[1,64,128]{2,1,0:T(8,128)S(1)} %get-tuple-element.93), channel_id=1, source_target_pairs={{1,0},{2,1},{3,2},{4,3},{5,4},{6,5},{7,6},{8,7},{9,8},{10,9},{11,1... | collective-permute-start | bytes 98312 | tf_op jit(solution)/shard_map/ppermute | solution.py:23
  14.2 29.7 %copy-start.6 = (f32[1,4,2,64,128]{4,1,3,2,0:T(4,128)}, f32[1,4,2,64,128]{4,1,3,2,0:T(4,128)S(1)}, u32[]{:S(2)}) copy-start(f32[1,4,2,64,128]{4,1,3,2,0:T(4,128)S(1)} %copy.36) | copy-start | bytes 786436
  14.2 29.0 %collective-permute-start.13 = (f32[4,1,64,128]{3,0,2,1:T(4,128)S(1)}, f32[4,1,64,128]{3,0,2,1:T(4,128)S(1)}, u32[]{:S(2)}, u32[]{:S(2)}) collective-permute-start(f32[4,1,64,128]{3,0,2,1:T(4,128)S(1)} %get-tuple-element.78), channel_id=1, source_target_pairs={{0,1},{1,2},{2,3},{3,4},{4,5},{5,6},{6,7},{7,8},{8,9},{9,10},{10,1... | collective-permute-start | bytes 393224 | tf_op jit(solution)/shard_map/ppermute | solution.py:20
  18.8 24.5 %collective-permute-start.12 = (f32[4,1,64,128]{3,0,2,1:T(4,128)S(1)}, f32[4,1,64,128]{3,0,2,1:T(4,128)S(1)}, u32[]{:S(2)}, u32[]{:S(2)}) collective-permute-start(f32[4,1,64,128]{3,0,2,1:T(4,128)S(1)} %get-tuple-element.79), channel_id=1, source_target_pairs={{1,0},{2,1},{3,2},{4,3},{5,4},{6,5},{7,6},{8,7},{9,8},{10,9},{11,1... | collective-permute-start | bytes 393224 | tf_op jit(solution)/shard_map/ppermute | solution.py:23
  20.3 8.4 %collective-permute-start.3 = (f32[4,1,64,128]{3,0,2,1:T(4,128)S(1)}, f32[4,1,64,128]{3,0,2,1:T(4,128)S(1)}, u32[]{:S(2)}, u32[]{:S(2)}) collective-permute-start(f32[4,1,64,128]{3,0,2,1:T(4,128)S(1)} %get-tuple-element.88), channel_id=1, source_target_pairs={{0,1},{1,2},{2,3},{3,4},{4,5},{5,6},{6,7},{7,8},{8,9},{9,10},{10,1... | collective-permute-start | bytes 393224 | tf_op jit(solution)/shard_map/ppermute | solution.py:20
  27.0 6.9 %collective-permute-start.1 = (f32[4,1,64,128]{3,0,2,1:T(4,128)S(1)}, f32[4,1,64,128]{3,0,2,1:T(4,128)S(1)}, u32[]{:S(2)}, u32[]{:S(2)}) collective-permute-start(f32[4,1,64,128]{3,0,2,1:T(4,128)S(1)} %get-tuple-element.89), channel_id=1, source_target_pairs={{1,0},{2,1},{3,2},{4,3},{5,4},{6,5},{7,6},{8,7},{9,8},{10,9},{11,1... | collective-permute-start | bytes 393224 | tf_op jit(solution)/shard_map/ppermute | solution.py:23
  28.6 15.2 %copy-start.58 = (f32[2,64,128]{2,1,0:T(8,128)}, f32[2,64,128]{2,1,0:T(8,128)S(1)}, u32[]{:S(2)}) copy-start(f32[2,64,128]{2,1,0:T(8,128)S(1)} %get-tuple-element.66) | copy-start | bytes 196612
  28.7 15.2 %copy-start.64 = (f32[2,64,128]{2,1,0:T(8,128)}, f32[2,64,128]{2,1,0:T(8,128)S(1)}, u32[]{:S(2)}) copy-start(f32[2,64,128]{2,1,0:T(8,128)S(1)} %get-tuple-element.67) | copy-start | bytes 196612
  28.7 15.2 %copy-start.70 = (f32[2,64,128]{2,1,0:T(8,128)}, f32[2,64,128]{2,1,0:T(8,128)S(1)}, u32[]{:S(2)}) copy-start(f32[2,64,128]{2,1,0:T(8,128)S(1)} %get-tuple-element.68) | copy-start | bytes 196612
  28.7 15.2 %copy-start.76 = (f32[2,64,128]{2,1,0:T(8,128)}, f32[2,64,128]{2,1,0:T(8,128)S(1)}, u32[]{:S(2)}) copy-start(f32[2,64,128]{2,1,0:T(8,128)S(1)} %get-tuple-element.69) | copy-start | bytes 196612
  28.7 15.2 %copy-start.82 = (f32[2,64,128]{2,1,0:T(8,128)}, f32[2,64,128]{2,1,0:T(8,128)S(1)}, u32[]{:S(2)}) copy-start(f32[2,64,128]{2,1,0:T(8,128)S(1)} %get-tuple-element.90) | copy-start | bytes 196612
  28.7 15.2 %copy-start.88 = (f32[2,64,128]{2,1,0:T(8,128)}, f32[2,64,128]{2,1,0:T(8,128)S(1)}, u32[]{:S(2)}) copy-start(f32[2,64,128]{2,1,0:T(8,128)S(1)} %get-tuple-element.91) | copy-start | bytes 196612
  36.9 17.5 %collective-permute-start.5 = (f32[4,1,64,128]{3,0,2,1:T(4,128)S(1)}, f32[4,1,64,128]{3,0,2,1:T(4,128)S(1)}, u32[]{:S(2)}, u32[]{:S(2)}) collective-permute-start(f32[4,1,64,128]{3,0,2,1:T(4,128)S(1)} %get-tuple-element.86), channel_id=1, source_target_pairs={{0,1},{1,2},{2,3},{3,4},{4,5},{5,6},{6,7},{7,8},{8,9},{9,10},{10,1... | collective-permute-start | bytes 393224 | tf_op jit(solution)/shard_map/ppermute | solution.py:20
  41.9 12.6 %collective-permute-start.4 = (f32[4,1,64,128]{3,0,2,1:T(4,128)S(1)}, f32[4,1,64,128]{3,0,2,1:T(4,128)S(1)}, u32[]{:S(2)}, u32[]{:S(2)}) collective-permute-start(f32[4,1,64,128]{3,0,2,1:T(4,128)S(1)} %get-tuple-element.87), channel_id=1, source_target_pairs={{1,0},{2,1},{3,2},{4,3},{5,4},{6,5},{7,6},{8,7},{9,8},{10,9},{11,1... | collective-permute-start | bytes 393224 | tf_op jit(solution)/shard_map/ppermute | solution.py:23
  43.9 10.6 %copy-start.9 = (f32[4,2,64,128]{3,0,2,1:T(4,128)S(1)}, f32[4,2,64,128]{3,0,2,1:T(4,128)}, u32[]{:S(2)}) copy-start(f32[4,2,64,128]{3,0,2,1:T(4,128)} %copy-done.8) | copy-start | bytes 786436
  45.1 10.0 %copy-start.59 = (f32[2,64,128]{2,1,0:T(8,128)S(1)}, f32[2,64,128]{2,1,0:T(8,128)}, u32[]{:S(2)}) copy-start(f32[2,64,128]{2,1,0:T(8,128)} %copy-done.58) | copy-start | bytes 196612
  45.1 10.0 %copy-start.65 = (f32[2,64,128]{2,1,0:T(8,128)S(1)}, f32[2,64,128]{2,1,0:T(8,128)}, u32[]{:S(2)}) copy-start(f32[2,64,128]{2,1,0:T(8,128)} %copy-done.64) | copy-start | bytes 196612
  45.1 10.0 %copy-start.71 = (f32[2,64,128]{2,1,0:T(8,128)S(1)}, f32[2,64,128]{2,1,0:T(8,128)}, u32[]{:S(2)}) copy-start(f32[2,64,128]{2,1,0:T(8,128)} %copy-done.70) | copy-start | bytes 196612
  45.8 23.0 %collective-permute-start.15 = (f32[4,1,64,128]{3,0,2,1:T(4,128)}, f32[4,1,64,128]{3,0,2,1:T(4,128)}, u32[]{:S(2)}, u32[]{:S(2)}) collective-permute-start(f32[4,1,64,128]{3,0,2,1:T(4,128)} %get-tuple-element.76), channel_id=1, source_target_pairs={{0,1},{1,2},{2,3},{3,4},{4,5},{5,6},{6,7},{7,8},{8,9},{9,10},{10,1... | collective-permute-start | bytes 393224 | tf_op jit(solution)/shard_map/ppermute | solution.py:20
  53.1 15.7 %collective-permute-start.14 = (f32[4,1,64,128]{3,0,2,1:T(4,128)}, f32[4,1,64,128]{3,0,2,1:T(4,128)}, u32[]{:S(2)}, u32[]{:S(2)}) collective-permute-start(f32[4,1,64,128]{3,0,2,1:T(4,128)} %get-tuple-element.77), channel_id=1, source_target_pairs={{1,0},{2,1},{3,2},{4,3},{5,4},{6,5},{7,6},{8,7},{9,8},{10,9},{11,1... | collective-permute-start | bytes 393224 | tf_op jit(solution)/shard_map/ppermute | solution.py:23
  60.4 10.1 %copy-start.20 = (f32[4,2,64,128]{3,0,2,1:T(4,128)S(1)}, f32[4,2,64,128]{3,0,2,1:T(4,128)}, u32[]{:S(2)}) copy-start(f32[4,2,64,128]{3,0,2,1:T(4,128)} %copy-done.19) | copy-start | bytes 786436
  60.4 10.1 %copy-start.60 = (f32[2,64,128]{2,1,0:T(8,128)S(1)}, f32[2,64,128]{2,1,0:T(8,128)}, u32[]{:S(2)}) copy-start(f32[2,64,128]{2,1,0:T(8,128)} %copy-done.58) | copy-start | bytes 196612
  60.4 10.1 %copy-start.66 = (f32[2,64,128]{2,1,0:T(8,128)S(1)}, f32[2,64,128]{2,1,0:T(8,128)}, u32[]{:S(2)}) copy-start(f32[2,64,128]{2,1,0:T(8,128)} %copy-done.64) | copy-start | bytes 196612
  60.4 10.1 %copy-start.72 = (f32[2,64,128]{2,1,0:T(8,128)S(1)}, f32[2,64,128]{2,1,0:T(8,128)}, u32[]{:S(2)}) copy-start(f32[2,64,128]{2,1,0:T(8,128)} %copy-done.70) | copy-start | bytes 196612
  60.5 10.1 %copy-start.78 = (f32[2,64,128]{2,1,0:T(8,128)S(1)}, f32[2,64,128]{2,1,0:T(8,128)}, u32[]{:S(2)}) copy-start(f32[2,64,128]{2,1,0:T(8,128)} %copy-done.76) | copy-start | bytes 196612
  60.5 10.1 %copy-start.84 = (f32[2,64,128]{2,1,0:T(8,128)S(1)}, f32[2,64,128]{2,1,0:T(8,128)}, u32[]{:S(2)}) copy-start(f32[2,64,128]{2,1,0:T(8,128)} %copy-done.82) | copy-start | bytes 196612
  60.5 10.1 %copy-start.90 = (f32[2,64,128]{2,1,0:T(8,128)S(1)}, f32[2,64,128]{2,1,0:T(8,128)}, u32[]{:S(2)}) copy-start(f32[2,64,128]{2,1,0:T(8,128)} %copy-done.88) | copy-start | bytes 196612
  61.5 19.1 %collective-permute-start.7 = (f32[4,1,64,128]{3,0,2,1:T(4,128)S(1)}, f32[4,1,64,128]{3,0,2,1:T(4,128)S(1)}, u32[]{:S(2)}, u32[]{:S(2)}) collective-permute-start(f32[4,1,64,128]{3,0,2,1:T(4,128)S(1)} %get-tuple-element.84), channel_id=1, source_target_pairs={{0,1},{1,2},{2,3},{3,4},{4,5},{5,6},{6,7},{7,8},{8,9},{9,10},{10,1... | collective-permute-start | bytes 393224 | tf_op jit(solution)/shard_map/ppermute | solution.py:20
  67.6 13.1 %collective-permute-start.6 = (f32[4,1,64,128]{3,0,2,1:T(4,128)S(1)}, f32[4,1,64,128]{3,0,2,1:T(4,128)S(1)}, u32[]{:S(2)}, u32[]{:S(2)}) collective-permute-start(f32[4,1,64,128]{3,0,2,1:T(4,128)S(1)} %get-tuple-element.85), channel_id=1, source_target_pairs={{1,0},{2,1},{3,2},{4,3},{5,4},{6,5},{7,6},{8,7},{9,8},{10,9},{11,1... | collective-permute-start | bytes 393224 | tf_op jit(solution)/shard_map/ppermute | solution.py:23
  70.6 10.1 %copy-start.12 = (f32[4,2,64,128]{3,0,2,1:T(4,128)S(1)}, f32[4,2,64,128]{3,0,2,1:T(4,128)}, u32[]{:S(2)}) copy-start(f32[4,2,64,128]{3,0,2,1:T(4,128)} %scatter-add.25) | copy-start | bytes 786436
  74.0 19.6 %collective-permute-start.17 = (f32[4,1,64,128]{3,0,2,1:T(4,128)}, f32[4,1,64,128]{3,0,2,1:T(4,128)}, u32[]{:S(2)}, u32[]{:S(2)}) collective-permute-start(f32[4,1,64,128]{3,0,2,1:T(4,128)} %get-tuple-element.74), channel_id=1, source_target_pairs={{0,1},{1,2},{2,3},{3,4},{4,5},{5,6},{6,7},{7,8},{8,9},{9,10},{10,1... | collective-permute-start | bytes 393224 | tf_op jit(solution)/shard_map/ppermute | solution.py:20
  79.2 14.4 %collective-permute-start.16 = (f32[4,1,64,128]{3,0,2,1:T(4,128)}, f32[4,1,64,128]{3,0,2,1:T(4,128)}, u32[]{:S(2)}, u32[]{:S(2)}) collective-permute-start(f32[4,1,64,128]{3,0,2,1:T(4,128)} %get-tuple-element.75), channel_id=1, source_target_pairs={{1,0},{2,1},{3,2},{4,3},{5,4},{6,5},{7,6},{8,7},{9,8},{10,9},{11,1... | collective-permute-start | bytes 393224 | tf_op jit(solution)/shard_map/ppermute | solution.py:23
  87.7 21.4 %collective-permute-start.9 = (f32[4,1,64,128]{3,0,2,1:T(4,128)S(1)}, f32[4,1,64,128]{3,0,2,1:T(4,128)S(1)}, u32[]{:S(2)}, u32[]{:S(2)}) collective-permute-start(f32[4,1,64,128]{3,0,2,1:T(4,128)S(1)} %get-tuple-element.82), channel_id=1, source_target_pairs={{0,1},{1,2},{2,3},{3,4},{4,5},{5,6},{6,7},{7,8},{8,9},{9,10},{10,1... | collective-permute-start | bytes 393224 | tf_op jit(solution)/shard_map/ppermute | solution.py:20
  92.3 16.9 %collective-permute-start.8 = (f32[4,1,64,128]{3,0,2,1:T(4,128)S(1)}, f32[4,1,64,128]{3,0,2,1:T(4,128)S(1)}, u32[]{:S(2)}, u32[]{:S(2)}) collective-permute-start(f32[4,1,64,128]{3,0,2,1:T(4,128)S(1)} %get-tuple-element.83), channel_id=1, source_target_pairs={{1,0},{2,1},{3,2},{4,3},{5,4},{6,5},{7,6},{8,7},{9,8},{10,9},{11,1... | collective-permute-start | bytes 393224 | tf_op jit(solution)/shard_map/ppermute | solution.py:23
  95.4 11.3 %copy-start.5 = (f32[4,4,66,130]{3,0,2,1:T(4,128)S(1)}, f32[4,4,66,130]{3,0,2,1:T(4,128)}, u32[]{:S(2)}) copy-start(f32[4,4,66,130]{3,0,2,1:T(4,128)} %copy-done.4) | copy-start | bytes 1647364
  95.4 11.3 %copy-start.13 = (f32[4,2,64,128]{3,0,2,1:T(4,128)S(1)}, f32[4,2,64,128]{3,0,2,1:T(4,128)}, u32[]{:S(2)}) copy-start(f32[4,2,64,128]{3,0,2,1:T(4,128)} %scatter-add.25) | copy-start | bytes 786436
  95.4 11.3 %copy-start.51 = (f32[4,1,64,128]{3,0,2,1:T(4,128)S(1)}, f32[4,1,64,128]{3,0,2,1:T(4,128)}, u32[]{:S(2)}) copy-start(f32[4,1,64,128]{3,0,2,1:T(4,128)} %copy-done.50) | copy-start | bytes 393220
  95.4 11.3 %copy-start.55 = (f32[4,1,64,128]{3,0,2,1:T(4,128)S(1)}, f32[4,1,64,128]{3,0,2,1:T(4,128)}, u32[]{:S(2)}) copy-start(f32[4,1,64,128]{3,0,2,1:T(4,128)} %copy-done.54) | copy-start | bytes 393220
  98.4 25.1 %collective-permute-start.19 = (f32[4,1,64,128]{3,0,2,1:T(4,128)}, f32[4,1,64,128]{3,0,2,1:T(4,128)}, u32[]{:S(2)}, u32[]{:S(2)}) collective-permute-start(f32[4,1,64,128]{3,0,2,1:T(4,128)} %get-tuple-element.72), channel_id=1, source_target_pairs={{0,1},{1,2},{2,3},{3,4},{4,5},{5,6},{6,7},{7,8},{8,9},{9,10},{10,1... | collective-permute-start | bytes 393224 | tf_op jit(solution)/shard_map/ppermute | solution.py:20
  105.2 18.4 %collective-permute-start.18 = (f32[4,1,64,128]{3,0,2,1:T(4,128)}, f32[4,1,64,128]{3,0,2,1:T(4,128)}, u32[]{:S(2)}, u32[]{:S(2)}) collective-permute-start(f32[4,1,64,128]{3,0,2,1:T(4,128)} %get-tuple-element.73), channel_id=1, source_target_pairs={{1,0},{2,1},{3,2},{4,3},{5,4},{6,5},{7,6},{8,7},{9,8},{10,9},{11,1... | collective-permute-start | bytes 393224 | tf_op jit(solution)/shard_map/ppermute | solution.py:23
  115.1 10.1 %copy-start.25 = (f32[4,2,64,128]{3,0,2,1:T(4,128)S(1)}, f32[4,2,64,128]{3,0,2,1:T(4,128)}, u32[]{:S(2)}) copy-start(f32[4,2,64,128]{3,0,2,1:T(4,128)} %copy-done.24) | copy-start | bytes 786436
  115.1 10.1 %copy-start.62 = (f32[2,64,128]{2,1,0:T(8,128)S(1)}, f32[2,64,128]{2,1,0:T(8,128)}, u32[]{:S(2)}) copy-start(f32[2,64,128]{2,1,0:T(8,128)} %copy-done.58) | copy-start | bytes 196612
  115.1 10.2 %copy-start.68 = (f32[2,64,128]{2,1,0:T(8,128)S(1)}, f32[2,64,128]{2,1,0:T(8,128)}, u32[]{:S(2)}) copy-start(f32[2,64,128]{2,1,0:T(8,128)} %copy-done.64) | copy-start | bytes 196612
  115.1 10.2 %copy-start.74 = (f32[2,64,128]{2,1,0:T(8,128)S(1)}, f32[2,64,128]{2,1,0:T(8,128)}, u32[]{:S(2)}) copy-start(f32[2,64,128]{2,1,0:T(8,128)} %copy-done.70) | copy-start | bytes 196612
  115.1 10.2 %copy-start.80 = (f32[2,64,128]{2,1,0:T(8,128)S(1)}, f32[2,64,128]{2,1,0:T(8,128)}, u32[]{:S(2)}) copy-start(f32[2,64,128]{2,1,0:T(8,128)} %copy-done.76) | copy-start | bytes 196612
  115.1 10.2 %copy-start.86 = (f32[2,64,128]{2,1,0:T(8,128)S(1)}, f32[2,64,128]{2,1,0:T(8,128)}, u32[]{:S(2)}) copy-start(f32[2,64,128]{2,1,0:T(8,128)} %copy-done.82) | copy-start | bytes 196612
  115.2 10.2 %copy-start.92 = (f32[2,64,128]{2,1,0:T(8,128)S(1)}, f32[2,64,128]{2,1,0:T(8,128)}, u32[]{:S(2)}) copy-start(f32[2,64,128]{2,1,0:T(8,128)} %copy-done.88) | copy-start | bytes 196612
  116.2 23.8 %collective-permute-start.11 = (f32[4,1,64,128]{3,0,2,1:T(4,128)S(1)}, f32[4,1,64,128]{3,0,2,1:T(4,128)S(1)}, u32[]{:S(2)}, u32[]{:S(2)}) collective-permute-start(f32[4,1,64,128]{3,0,2,1:T(4,128)S(1)} %get-tuple-element.80), channel_id=1, source_target_pairs={{0,1},{1,2},{2,3},{3,4},{4,5},{5,6},{6,7},{7,8},{8,9},{9,10},{10,1... | collective-permute-start | bytes 393224 | tf_op jit(solution)/shard_map/ppermute | solution.py:20
  122.3 17.7 %collective-permute-start.10 = (f32[4,1,64,128]{3,0,2,1:T(4,128)S(1)}, f32[4,1,64,128]{3,0,2,1:T(4,128)S(1)}, u32[]{:S(2)}, u32[]{:S(2)}) collective-permute-start(f32[4,1,64,128]{3,0,2,1:T(4,128)S(1)} %get-tuple-element.81), channel_id=1, source_target_pairs={{1,0},{2,1},{3,2},{4,3},{5,4},{6,5},{7,6},{8,7},{9,8},{10,9},{11,1... | collective-permute-start | bytes 393224 | tf_op jit(solution)/shard_map/ppermute | solution.py:23
  125.3 10.8 %copy-start.1 = (f32[4,4,66,130]{3,0,2,1:T(4,128)S(1)}, f32[4,4,66,130]{3,0,2,1:T(4,128)}, u32[]{:S(2)}) copy-start(f32[4,4,66,130]{3,0,2,1:T(4,128)} %copy-done) | copy-start | bytes 1647364
  125.3 10.8 %copy-start.3 = (f32[4,4,66,130]{3,0,2,1:T(4,128)S(1)}, f32[4,4,66,130]{3,0,2,1:T(4,128)}, u32[]{:S(2)}) copy-start(f32[4,4,66,130]{3,0,2,1:T(4,128)} %copy-done.2) | copy-start | bytes 1647364
  125.3 10.8 %copy-start.16 = (f32[4,2,64,128]{3,0,2,1:T(4,128)S(1)}, f32[4,2,64,128]{3,0,2,1:T(4,128)}, u32[]{:S(2)}) copy-start(f32[4,2,64,128]{3,0,2,1:T(4,128)} %scatter-add.26) | copy-start | bytes 786436
  125.3 10.8 %copy-start.21 = (f32[4,2,64,128]{3,0,2,1:T(4,128)S(1)}, f32[4,2,64,128]{3,0,2,1:T(4,128)}, u32[]{:S(2)}) copy-start(f32[4,2,64,128]{3,0,2,1:T(4,128)} %copy-done.19) | copy-start | bytes 786436
  125.4 10.8 %copy-start.43 = (f32[4,1,64,128]{3,0,2,1:T(4,128)S(1)}, f32[4,1,64,128]{3,0,2,1:T(4,128)}, u32[]{:S(2)}) copy-start(f32[4,1,64,128]{3,0,2,1:T(4,128)} %copy-done.42) | copy-start | bytes 393220
  125.4 10.8 %copy-start.46 = (f32[4,1,64,128]{3,0,2,1:T(4,128)S(1)}, f32[4,1,64,128]{3,0,2,1:T(4,128)}, u32[]{:S(2)}) copy-start(f32[4,1,64,128]{3,0,2,1:T(4,128)} %copy-done.45) | copy-start | bytes 393220
  127.7 16.5 %copy-start.22 = (f32[4,2,64,128]{3,0,2,1:T(4,128)}, f32[4,2,64,128]{3,0,2,1:T(4,128)S(1)}, u32[]{:S(2)}) copy-start(f32[4,2,64,128]{3,0,2,1:T(4,128)S(1)} %fusion.4) | copy-start | bytes 786436
  127.7 14.3 %collective-permute-start.21 = (f32[4,1,64,128]{3,0,2,1:T(4,128)S(1)}, f32[4,1,64,128]{3,0,2,1:T(4,128)S(1)}, u32[]{:S(2)}, u32[]{:S(2)}) collective-permute-start(f32[4,1,64,128]{3,0,2,1:T(4,128)S(1)} %get-tuple-element.70), channel_id=1, source_target_pairs={{0,1},{1,2},{2,3},{3,4},{4,5},{5,6},{6,7},{7,8},{8,9},{9,10},{10,1... | collective-permute-start | bytes 393224 | tf_op jit(solution)/shard_map/ppermute | solution.py:20
  134.4 9.1 %collective-permute-start.20 = (f32[4,1,64,128]{3,0,2,1:T(4,128)S(1)}, f32[4,1,64,128]{3,0,2,1:T(4,128)S(1)}, u32[]{:S(2)}, u32[]{:S(2)}) collective-permute-start(f32[4,1,64,128]{3,0,2,1:T(4,128)S(1)} %get-tuple-element.71), channel_id=1, source_target_pairs={{1,0},{2,1},{3,2},{4,3},{5,4},{6,5},{7,6},{8,7},{9,8},{10,9},{11,1... | collective-permute-start | bytes 393224 | tf_op jit(solution)/shard_map/ppermute | solution.py:23
  (56 other events, 212.9 us)
Sparse Core Ops, SparseCore 0:
  145.9 128.7 all-reduce.12
where the time goes:
time: 472 us; the launch traced here: 471 us
  other arithmetic  135 us (29%)
  waiting for transfers between devices  129 us (27%)
  blocking collectives  75.4 us (16%)
  starting transfers between devices  75.2 us (16%)
  local copies, waits for them, and re-layouts  23 us (5%)
  between operations  17.9 us (4%)
  matrix products  15.3 us (3%)
    psum x1, waiting for transfers between devices, on_device(): summed = lax.psum(weighted, 'exp')  122 us
    scatter-add x1, other arithmetic, on_device(): jax.ops.segment_sum(summed.reshape(-1), flat_labels, num_segments=LABELS)  114 us
    psum x1, blocking collectives, on_device(): total = lax.psum(binned, 'space')  75.4 us
    ppermute x11, starting transfers between devices, extended(): lax.ppermute(lax.slice_in_dim(block, block.shape[dim] - width, None, axis...  60.2 us
    ppermute x11, starting transfers between devices, extended(): lax.ppermute(lax.slice_in_dim(block, 0, width, axis=dim), axis, backward)  15 us
    scatter-add x5, local copies, waits for them, and re-layouts, on_device(): state = state.at[0].add(pulse)  11 us
  transfers between devices with their start and end apart: 23, of which 3 were waited for; matrix products, arithmetic and copies ran while one was open for 11% of the time, Pallas kernels for 0%

commit v1 on v0

v1 whole, which is shorter than its diff:
```python
import math

import jax
import jax.numpy as jnp
from jax import lax
from jax.experimental import pallas as pl
from jax.experimental.pallas import tpu as pltpu
from jax.sharding import PartitionSpec as P

STEPS = 5
LABELS = 512
TAU = 0.1
ROWS = 16
F32 = jnp.float32

A_AT, TS_AT, S_AT, LO_AT, HI_AT, DOSE_AT, NORM_AT = 0, 32, 36, 40, 41, 42, 43


def coupling(coupling_mask, coupling_rate):
    size = coupling_rate.shape[0]
    off = coupling_mask.astype(F32) * coupling_rate * (1.0 - jnp.eye(size, dtype=F32))
    return off - jnp.diag(jnp.sum(off, axis=1))


def up(ref, index, r, rows):
    if r + rows < ref.shape[-2]:
        return ref[(*index, pl.ds(r + 1, rows), slice(None))]
    return pltpu.roll(ref[(*index, pl.ds(r, rows), slice(None))], rows - 1, 0)


def down(ref, index, r, rows):
    if r > 0:
        return ref[(*index, pl.ds(r - 1, rows), slice(None))]
    return pltpu.roll(ref[(*index, pl.ds(r, rows), slice(None))], 1, 0)


def face_weights(planes, coef):
    wide, deep = coef.shape[-2:]
    row = lax.broadcasted_iota(jnp.int32, (wide, deep), 0)
    lane = lax.broadcasted_iota(jnp.int32, (wide, deep), 1)
    edges = (
        (row == 0).astype(F32)
        + (row == wide - 1).astype(F32)
        + (lane == 0).astype(F32)
        + (lane == deep - 1).astype(F32)
    )
    half = [0.5 * p for p in planes]
    for j in range(1, len(planes) - 1):
        h = half[j]
        zp = jnp.where(lane == deep - 1, 0.0, h + pltpu.roll(h, deep - 1, 1))
        yp = jnp.where(row == wide - 1, 0.0, h + pltpu.roll(h, wide - 1, 0))
        zm = pltpu.roll(zp, 1, 1)
        ym = pltpu.roll(yp, 1, 0)
        xp = h + half[j + 1]
        xm = h + half[j - 1]
        out = (zp, zm, yp, ym, xp, xm, zp + zm + yp + ym + xp + xm + edges * h)
        for k, value in enumerate(out):
            coef[j - 1, k] = value


def advance(f, step_of_u, get, put, coef, first, count, fl, it):
    wide, deep = coef.shape[-2:]
    offset = coef.shape[0] // 2 - 1
    for j in range(first, first + count):
        on = (f == 0) & (it[2] <= step_of_u) & (it[0] == j)
        amp = jnp.where(on, fl[DOSE_AT], 0.0)
        for r in range(0, wide, ROWS):
            rows = pl.ds(r, ROWS)
            zp, zm, yp, ym, xp, xm, total = [coef[j + offset, k, rows, :] for k in range(7)]
            center = []
            for c in range(4):
                ref, index = get(c, j)
                center.append(ref[(*index, rows, slice(None))])
            for c in range(4):
                ref, index = get(c, j)
                v = center[c]
                ref_up, index_up = get(c, j + 1)
                ref_dn, index_dn = get(c, j - 1)
                flow = zp * pltpu.roll(v, deep - 1, 1) + zm * pltpu.roll(v, 1, 1)
                flow = flow + (yp * up(ref, index, r, ROWS) + ym * down(ref, index, r, ROWS))
                flow = flow + (
                    xp * ref_up[(*index_up, rows, slice(None))]
                    + xm * ref_dn[(*index_dn, rows, slice(None))]
                )
                flow = flow - total * v
                new = fl[TS_AT + c] * flow
                for d in range(4):
                    new = new + fl[A_AT + f * 16 + c * 4 + d] * center[d]
                if c == 0:
                    at = (
                        lax.broadcasted_iota(jnp.int32, (ROWS, deep), 0) + r
                    ) * deep + lax.broadcasted_iota(jnp.int32, (ROWS, deep), 1)
                    new = new + jnp.where(at == it[1], amp, 0.0)
                if j < 0:
                    new = new * fl[LO_AT]
                if j > 1:
                    new = new * fl[HI_AT]
                out, index_out = put(c, j)
                out[(*index_out, rows, slice(None))] = new


def two_steps(first_step, perm_at):
    def kernel(fl, it, own, low, high, plow, pmid, phigh, mid, *rest):
        out, coef = rest[:-1], rest[-1]
        planes = [plow[(*perm_at, 0)], plow[(*perm_at, 1)], pmid[0], pmid[1]]
        planes += [phigh[(*perm_at, 0)], phigh[(*perm_at, 1)]]
        face_weights(planes, coef)

        def field(f, carry):
            def source(c, j):
                k = f * 4 + c
                if j < 0:
                    return low, (k, j + 2)
                if j > 1:
                    return high, (k, j - 2)
                return own, (k, j)

            def middle(c, j):
                return mid, (f * 4 + c, j + 1)

            def last(c, j):
                if len(out) == 1:
                    return out[0], (f * 4 + c, j)
                return out[j], (f * 4 + c,)

            advance(f, first_step, source, middle, coef, -1, 4, fl, it)
            advance(f, first_step + 1, middle, last, coef, 0, 2, fl, it)
            return carry

        lax.fori_loop(0, 2, field, 0)

    return kernel


def gradient(fl, s0, t1, s2, low2, high2, t3, s4a, s4b, out, fz, fy, fb):
    wide, deep = out.shape[-2:]

    def plane(stage, f, c, j):
        k = f * 4 + c
        if stage == 0:
            return s0, (k, j)
        if stage == 1:
            return t1, (k, j + 1)
        if stage == 3:
            return t3, (k, j + 1)
        if stage == 4:
            return (s4a, (k,)) if j == 0 else (s4b, (k,))
        if j < 0:
            return low2, (k, 1)
        if j > 1:
            return high2, (k, 0)
        return s2, (k, j)

    for r in range(0, wide, ROWS):
        rows = pl.ds(r, ROWS)
        x_low = x_mid = x_high = jnp.zeros((ROWS, deep), F32)
        acc_z, acc_y, acc_b = [[jnp.zeros((ROWS, deep), F32)] * 2 for _ in range(3)]
        for n in range(STEPS):
            for c in range(4):
                def load(f, j):
                    ref, index = plane(n if f == 0 else STEPS - 1 - n, f, c, j)
                    return ref[(*index, rows, slice(None))]

                def load_up(f, j):
                    ref, index = plane(n if f == 0 else STEPS - 1 - n, f, c, j)
                    return up(ref, index, r, ROWS)

                weight = fl[S_AT + c]
                u = [load(0, 0), load(0, 1)]
                l = [load(1, 0), load(1, 1)]
                w = [l[0] * weight, l[1] * weight]
                for j in range(2):
                    acc_b[j] = acc_b[j] + w[j] * u[j]
                    acc_z[j] = acc_z[j] + (pltpu.roll(w[j], deep - 1, 1) - w[j]) * (
                        pltpu.roll(u[j], deep - 1, 1) - u[j]
                    )
                    acc_y[j] = acc_y[j] + (load_up(1, j) * weight - w[j]) * (load_up(0, j) - u[j])
                x_mid = x_mid + (w[1] - w[0]) * (u[1] - u[0])
                if 0 < n < STEPS - 1:
                    x_low = x_low + (load(1, -1) * weight - w[0]) * (load(0, -1) - u[0])
                    x_high = x_high + (load(1, 2) * weight - w[1]) * (load(0, 2) - u[1])
        out[0, rows, :] = x_low + x_mid
        out[1, rows, :] = x_high + x_mid
        for j in range(2):
            fz[j, rows, :] = acc_z[j]
            fy[j, rows, :] = acc_y[j]
            fb[j, rows, :] = acc_b[j]
    row = lax.broadcasted_iota(jnp.int32, (wide, deep), 0)
    lane = lax.broadcasted_iota(jnp.int32, (wide, deep), 1)
    for j in range(2):
        b = fb[j]
        z, y = fz[j], fy[j]
        total = out[j] + jnp.where(lane == deep - 1, b, z)
        total = total + jnp.where(lane == 0, b, pltpu.roll(z, 1, 1))
        total = total + jnp.where(row == wide - 1, b, y)
        total = total + jnp.where(row == 0, b, pltpu.roll(y, 1, 0))
        out[j] = total


def final(fl, it, s0, low0, high0, s4a, s4b, low4, high4, part, perm, labels, conc, sens, bins, coef):
    wide, deep = perm.shape[-2:]
    face_weights([low0[8, 1], perm[0], perm[1], high0[8, 0]], coef)

    def bin_rows(k, total):
        r = pl.multiple_of(k * 8, 8)
        rows = pl.ds(r, 8)
        for j in range(2):
            g = part[j, rows, :]
            for c in range(4):
                weight = fl[S_AT + c]
                u4, l1 = (s4a, s4b)[j][c, rows, :], (s4a, s4b)[j][4 + c, rows, :]
                far = (low4, high4)[j]
                u0, l5 = s0[c, j, rows, :], s0[4 + c, j, rows, :]
                far0, at = ((low0, 1), (high0, 0))[j]
                g = g + weight * (
                    (far[4 + c, rows, :] - l1) * (far0[c, at, rows, :] - u0)
                    + (far0[4 + c, at, rows, :] - l5) * (far[c, rows, :] - u4)
                )
            value = g * perm[j, rows, :] * fl[NORM_AT]
            label = labels[j, rows, :]
            coarse, fine = label >> 5, label & 31
            left, right = [], []
            for i in range(8):
                spread = jnp.broadcast_to(coarse[i : i + 1], (16, deep))
                hit = spread == lax.broadcasted_iota(jnp.int32, (16, deep), 0)
                left.append(jnp.where(hit, jnp.broadcast_to(value[i : i + 1], (16, deep)), 0.0))
                spread = jnp.broadcast_to(fine[i : i + 1], (32, deep))
                hit = spread == lax.broadcasted_iota(jnp.int32, (32, deep), 0)
                right.append(hit.astype(F32))
            total = total + lax.dot_general(
                jnp.concatenate(left, axis=1),
                jnp.concatenate(right, axis=1),
                (((1,), (1,)), ((), ())),
                precision=lax.Precision.HIGHEST,
                preferred_element_type=F32,
            )
        return total

    bins[...] = lax.fori_loop(0, wide // 8, bin_rows, jnp.zeros((16, 32), F32))

    for f, out in ((0, conc), (1, sens)):
        def source(c, j):
            k = f * 4 + c
            return (low4, s4a, s4b, high4)[j + 1], (k,)

        def target(c, j):
            return out, (c, j)

        advance(f, STEPS - 1, source, target, coef, 0, 2, fl, it)


SMEM = pl.BlockSpec(memory_space=pltpu.SMEM)
VMEM = pl.BlockSpec(memory_space=pltpu.VMEM)


def call(kernel, ins, scalars, outs, scratch, name, flops):
    size = sum(math.prod(x.shape) for x in ins) + sum(math.prod(s) for s in outs)
    return pl.pallas_call(
        kernel,
        out_shape=[jax.ShapeDtypeStruct(s, F32) for s in outs],
        in_specs=[SMEM] * len(scalars) + [VMEM] * len(ins),
        out_specs=[VMEM] * len(outs),
        scratch_shapes=[pltpu.VMEM(s, F32) for s in scratch],
        compiler_params=pltpu.CompilerParams(vmem_limit_bytes=24 << 20),
        cost_estimate=pl.CostEstimate(flops=flops, bytes_accessed=4 * size, transcendentals=0),
        name=name,
    )(*scalars, *ins)


def neighbours(block_low, block_high):
    count = lax.axis_size("space")
    forward = [(i, i + 1) for i in range(count - 1)]
    backward = [(target, source) for source, target in forward]
    return lax.ppermute(block_high, "space", forward), lax.ppermute(block_low, "space", backward)


def sum_over(x, axis, groups):
    n = len(groups[0])
    copies = jnp.broadcast_to(x[None], (n, *x.shape))
    got = lax.all_to_all(copies, axis, 0, 0, axis_index_groups=groups, tiled=True)
    return jnp.sum(got, axis=0)


def on_device(
    initial,
    cotangent,
    permeability,
    labels,
    comp_scale,
    coupling_mask,
    coupling_rate,
    dose,
    inject_voxel,
    arrival,
):
    rows, wide, deep = permeability.shape
    spaces, exps = lax.axis_size("space"), lax.axis_size("exp")
    here = lax.axis_index("space")
    mixing = coupling(coupling_mask, coupling_rate)
    eye = jnp.eye(4, dtype=F32)
    norm = math.sqrt(rows * spaces * wide * deep * exps / LABELS)
    fl = jnp.concatenate(
        [
            (eye + TAU * mixing).reshape(-1),
            (eye + TAU * mixing.T).reshape(-1),
            TAU * comp_scale,
            comp_scale,
            jnp.stack([(here > 0).astype(F32), (here < spaces - 1).astype(F32)]),
            TAU * dose,
            jnp.full((1,), -0.5 * TAU / norm, F32),
        ]
    )
    voxel = inject_voxel[0]
    it = jnp.stack([voxel // (wide * deep) - here * rows, voxel % (wide * deep), arrival[0]])

    s0 = jnp.concatenate([initial[0], cotangent[0], permeability[None]], axis=0)
    low0, high0 = neighbours(s0, s0)
    slab, plane = (8, 2, wide, deep), (8, wide, deep)
    coef = (4, 7, wide, deep)
    t1, s2 = call(
        two_steps(0, (8,)), [s0, low0, high0, low0, permeability, high0], [fl, it],
        [(8, 4, wide, deep), slab], [coef], "steps_1_2", 20_000_000,
    )
    low2, high2 = neighbours(s2, s2)
    t3, s4a, s4b = call(
        two_steps(2, (8,)), [s2, low2, high2, low0, permeability, high0], [fl, it],
        [(8, 4, wide, deep), plane, plane], [coef], "steps_3_4", 20_000_000,
    )
    low4, high4 = neighbours(s4a, s4b)
    part, = call(
        gradient, [s0, t1, s2, low2, high2, t3, s4a, s4b], [fl],
        [(2, wide, deep)], [(2, wide, deep)] * 3, "gradient", 10_000_000,
    )
    conc, sens, bins = call(
        final, [s0, low0, high0, s4a, s4b, low4, high4, part, permeability, labels], [fl, it],
        [(4, 2, wide, deep), (4, 2, wide, deep), (16, 32)], [(2, 7, wide, deep)], "final", 20_000_000,
    )
    bins = sum_over(bins, "exp", [list(range(exps))])
    near = 8 if spaces % 8 == 0 else spaces
    bins = sum_over(bins, "space", [[g * near + i for i in range(near)] for g in range(spaces // near)])
    if spaces > near:
        bins = sum_over(bins, "space", [[g * near + i for g in range(spaces // near)] for i in range(near)])
    return conc[None], sens[None], bins.reshape(-1)


def solution(mesh):
    return jax.shard_map(
        on_device,
        mesh=mesh,
        in_specs=(
            P("exp", None, "space", None, None),
            P("exp", None, "space", None, None),
            P("space", None, None),
            P("space", None, None),
            P(),
            P(),
            P(),
            P("exp"),
            P("exp"),
            P("exp"),
        ),
        out_specs=(P("exp", None, "space", None, None), P("exp", None, "space", None, None), P()),
        check_vma=False,
    )
```

time: 472 us -> 113 us (0.24)
  the two profiles are of different devices: /device:TPU:8 before, /device:TPU:2 now
where the time goes in v1:
time: 113 us; the launch traced here: 112 us
  blocking collectives  44.9 us (40%)
  waiting for transfers between devices  25.4 us (22%)
  starting transfers between devices  20.9 us (18%)
  Pallas kernels  11.1 us (10%)
  local copies, waits for them, and re-layouts  3.7 us (3%)
  other arithmetic  3.46 us (3%)
  between operations  2.82 us (2%)
    all_to_all x3, blocking collectives, sum_over(): lax.all_to_all(copies, axis, 0, 0, axis_index_groups=groups, tiled=True)  44.9 us
    ppermute x3, waiting for transfers between devices, neighbours(): lax.ppermute(block_high, 'space', forward)  12.7 us
    ppermute x3, waiting for transfers between devices, neighbours(): lax.ppermute(block_low, 'space', backward)  12.7 us
    pallas_call x4, Pallas kernels, call(): pl.pallas_call(kernel, out_shape=[jax.ShapeDtypeStruct(s, F32) for s in o...  11.1 us
    ppermute x3, starting transfers between devices, neighbours(): lax.ppermute(block_high, 'space', forward)  10.7 us
    ppermute x3, starting transfers between devices, neighbours(): lax.ppermute(block_low, 'space', backward)  10.2 us
  transfers between devices with their start and end apart: 6, of which 6 were waited for; matrix products, arithmetic and copies ran while one was open for 1% of the time, Pallas kernels for 2%

profile of v1, /device:TPU:2, one launch (start us, length us, event | category | flops | bytes accessed | tf_op | source)
XLA Modules:
  0.0 112.2 jit_solution(5949180489605658521)
XLA Ops:
  0.6 1.1 pad_maximum_fusion.own.s0
  1.7 3.4 %collective-permute-start = (f32[9,2,64,128]{3,2,1,0:T(8,128)S(1)}, f32[9,2,64,128]{3,2,1,0:T(8,128)S(1)}, u32[]{:S(2)}, u32[]{:S(2)}) collective-permute-start(f32[9,2,64,128]{3,2,1,0:T(8,128)S(1)} %pad_maximum_fusion.own.s0), channel_id=1, source_target_pairs={{0,1},{1,2},{2,3},{3,4},{4,5},{5,6},{6,7},{7,8},{8,9},{9,10},{10,1... | collective-permute-start | bytes 1769480 | tf_op jit(solution)/shard_map/ppermute | solution.py:274
  5.1 5.7 %collective-permute-start.1 = (f32[9,2,64,128]{3,2,1,0:T(8,128)S(1)}, f32[9,2,64,128]{3,2,1,0:T(8,128)S(1)}, u32[]{:S(2)}, u32[]{:S(2)}) collective-permute-start(f32[9,2,64,128]{3,2,1,0:T(8,128)S(1)} %pad_maximum_fusion.own.s0), channel_id=1, source_target_pairs={{1,0},{2,1},{3,2},{4,3},{5,4},{6,5},{7,6},{8,7},{9,8},{10,9},{11,1... | collective-permute-start | bytes 1769480 | tf_op jit(solution)/shard_map/ppermute | solution.py:274
  10.9 0.0 copy-start.2
  10.9 0.0 copy-start.3
  10.9 0.1 copy.18
  11.0 0.6 copy-done.2
  11.6 0.0 copy-done.3
  11.6 0.1 fusion.1
  11.7 0.0 copy-start
  11.7 0.1 copy.19
  13.2 0.1 copy.20
  13.3 0.1 copy.21
  13.4 0.1 reshape.19
  13.5 0.1 copy.22
  13.6 0.1 reshape.20
  14.3 0.0 copy-start.4
  14.3 0.6 copy-done.4
  15.0 0.1 concatenate.6.fl
  15.1 0.1 pad_add_fusion.it
  15.1 3.6 %collective-permute-done.low.plow.low0 = f32[9,2,64,128]{3,2,1,0:T(8,128)S(1)} collective-permute-done((f32[9,2,64,128]{3,2,1,0:T(8,128)S(1)}, f32[9,2,64,128]{3,2,1,0:T(8,128)S(1)}, u32[]{:S(2)}, u32[]{:S(2)}) %collective-permute-start) | collective-permute-done | bytes 589856 | tf_op jit(solution)/shard_map/ppermute | solution.py:274
  18.7 3.1 %collective-permute-done.1.high.phigh.high0 = f32[9,2,64,128]{3,2,1,0:T(8,128)S(1)} collective-permute-done((f32[9,2,64,128]{3,2,1,0:T(8,128)S(1)}, f32[9,2,64,128]{3,2,1,0:T(8,128)S(1)}, u32[]{:S(2)}, u32[]{:S(2)}) %collective-permute-start.1) | collective-permute-done | bytes 589856 | tf_op jit(solution)/shard_map/ppermute | solution.py:274
  21.8 0.0 copy-done
  21.8 2.2 %steps_1_2.1 = (f32[8,4,64,128]{3,2,1,0:T(8,128)S(1)}, f32[8,2,64,128]{3,2,1,0:T(8,128)S(1)}) custom-call(f32[44]{0:T(128)S(1)} %concatenate.6.fl, s32[3]{0:T(128)S(1)} %pad_add_fusion.it, f32[9,2,64,128]{3,2,1,0:T(8,128)S(1)} %pad_maximum_fusion.own.s0, f32[9,2,64,128]{3,2,1,0:T(8,128)S(1)} %collective-permute-done.low.plow.low0, ...), custom_call_target="tpu_custom_call" | custom-call | flops 20000000 | bytes 4587520 | tf_op jit(solution)/shard_map/steps_1_2/pallas_call | solution.py:258
  24.1 3.7 %collective-permute-start.2 = (f32[8,2,64,128]{3,2,1,0:T(8,128)S(1)}, f32[8,2,64,128]{3,2,1,0:T(8,128)S(1)}, u32[]{:S(2)}, u32[]{:S(2)}) collective-permute-start(f32[8,2,64,128]{3,2,1,0:T(8,128)S(1)} %get-tuple-element.11.own.s2), channel_id=1, source_target_pairs={{0,1},{1,2},{2,3},{3,4},{4,5},{5,6},{6,7},{7,8},{8,9},{9,10},{10,1... | collective-permute-start | bytes 1572872 | tf_op jit(solution)/shard_map/ppermute | solution.py:274
  27.7 2.2 %collective-permute-start.3 = (f32[8,2,64,128]{3,2,1,0:T(8,128)S(1)}, f32[8,2,64,128]{3,2,1,0:T(8,128)S(1)}, u32[]{:S(2)}, u32[]{:S(2)}) collective-permute-start(f32[8,2,64,128]{3,2,1,0:T(8,128)S(1)} %get-tuple-element.11.own.s2), channel_id=1, source_target_pairs={{1,0},{2,1},{3,2},{4,3},{5,4},{6,5},{7,6},{8,7},{9,8},{10,9},{11,1... | collective-permute-start | bytes 1572872 | tf_op jit(solution)/shard_map/ppermute | solution.py:274
  29.9 8.5 %collective-permute-done.2.low.low2 = f32[8,2,64,128]{3,2,1,0:T(8,128)S(1)} collective-permute-done((f32[8,2,64,128]{3,2,1,0:T(8,128)S(1)}, f32[8,2,64,128]{3,2,1,0:T(8,128)S(1)}, u32[]{:S(2)}, u32[]{:S(2)}) %collective-permute-start.2) | collective-permute-done | bytes 524320 | tf_op jit(solution)/shard_map/ppermute | solution.py:274
  38.4 5.5 %collective-permute-done.3.high.high2 = f32[8,2,64,128]{3,2,1,0:T(8,128)S(1)} collective-permute-done((f32[8,2,64,128]{3,2,1,0:T(8,128)S(1)}, f32[8,2,64,128]{3,2,1,0:T(8,128)S(1)}, u32[]{:S(2)}, u32[]{:S(2)}) %collective-permute-start.3) | collective-permute-done | bytes 524320 | tf_op jit(solution)/shard_map/ppermute | solution.py:274
  43.9 2.3 %steps_3_4.1 = (f32[8,4,64,128]{3,2,1,0:T(8,128)S(1)}, f32[8,64,128]{2,1,0:T(8,128)S(1)}, f32[8,64,128]{2,1,0:T(8,128)S(1)}) custom-call(f32[44]{0:T(128)S(1)} %concatenate.6.fl, s32[3]{0:T(128)S(1)} %pad_add_fusion.it, f32[8,2,64,128]{3,2,1,0:T(8,128)S(1)} %get-tuple-element.11.own.s2, f32[8,2,64,128]{3,2,1,0:T(8,128)S(1)} %collective-permute-done.2.low.low2, ...), custom_call_target="tpu_custom_call" | custom-call | flops 20000000 | bytes 4390912 | tf_op jit(solution)/shard_map/steps_3_4/pallas_call | solution.py:258
  46.3 3.6 %collective-permute-start.4 = (f32[8,64,128]{2,1,0:T(8,128)S(1)}, f32[8,64,128]{2,1,0:T(8,128)S(1)}, u32[]{:S(2)}, u32[]{:S(2)}) collective-permute-start(f32[8,64,128]{2,1,0:T(8,128)S(1)} %get-tuple-element.13.s4b), channel_id=1, source_target_pairs={{0,1},{1,2},{2,3},{3,4},{4,5},{5,6},{6,7},{7,8},{8,9},{9,10},{10,1... | collective-permute-start | bytes 786440 | tf_op jit(solution)/shard_map/ppermute | solution.py:274
  49.9 2.2 %collective-permute-start.5 = (f32[8,64,128]{2,1,0:T(8,128)S(1)}, f32[8,64,128]{2,1,0:T(8,128)S(1)}, u32[]{:S(2)}, u32[]{:S(2)}) collective-permute-start(f32[8,64,128]{2,1,0:T(8,128)S(1)} %get-tuple-element.12.s4a), channel_id=1, source_target_pairs={{1,0},{2,1},{3,2},{4,3},{5,4},{6,5},{7,6},{8,7},{9,8},{10,9},{11,1... | collective-permute-start | bytes 786440 | tf_op jit(solution)/shard_map/ppermute | solution.py:274
  52.1 0.0 copy-start.1
  52.1 1.7 %gradient.1.part = f32[2,64,128]{2,1,0:T(8,128)S(1)} custom-call(f32[44]{0:T(128)S(1)} %concatenate.6.fl, f32[9,2,64,128]{3,2,1,0:T(8,128)S(1)} %pad_maximum_fusion.own.s0, f32[8,4,64,128]{3,2,1,0:T(8,128)S(1)} %get-tuple-element.14.t1, f32[8,2,64,128]{3,2,1,0:T(8,128)S(1)} %get-tuple-element.11.own.s2, ...), custom_call_target="tpu_custom_call" | custom-call | flops 10000000 | bytes 4849664 | tf_op jit(solution)/shard_map/gradient/pallas_call | solution.py:258
  53.8 0.7 collective-permute-done.4.low4
  54.5 4.0 %collective-permute-done.5.high4 = f32[8,64,128]{2,1,0:T(8,128)S(1)} collective-permute-done((f32[8,64,128]{2,1,0:T(8,128)S(1)}, f32[8,64,128]{2,1,0:T(8,128)S(1)}, u32[]{:S(2)}, u32[]{:S(2)}) %collective-permute-start.5) | collective-permute-done | bytes 262176 | tf_op jit(solution)/shard_map/ppermute | solution.py:274
  58.6 0.0 copy-done.1
  58.6 4.9 %final.1 = (f32[4,2,64,128]{3,2,1,0:T(8,128)}, f32[4,2,64,128]{3,2,1,0:T(8,128)}, f32[16,32]{1,0:T(8,128)S(1)}) custom-call(f32[44]{0:T(128)S(1)} %concatenate.6.fl, s32[3]{0:T(128)S(1)} %pad_add_fusion.it, f32[9,2,64,128]{3,2,1,0:T(8,128)S(1)} %pad_maximum_fusion.own.s0, f32[9,2,64,128]{3,2,1,0:T(8,128)S(1)} %collective-permute-done.low.plow.low0, ...), custom_call_target="tpu_custom_call" | custom-call | flops 20000000 | bytes 3540992 | tf_op jit(solution)/shard_map/final/pallas_call | solution.py:258
  63.4 0.1 reshape.24
  63.6 14.7 %all_to_all.15 = f32[16,1,512]{2,1,0:T(1,128)S(1)} all-to-all(f32[16,1,512]{2,1,0:T(1,128)S(1)} %reshape.24), channel_id=1, replica_groups={{0,32,64,96,128,160,192,224,256,288,320,352,384,416,448,480},{1,33,65,9..., dimensions={0} | all-to-all | bytes 65536 | tf_op jit(solution)/shard_map/all_to_all | solution.py:280
  78.3 0.5 broadcast.24
  78.8 0.7 reduce
  79.5 0.1 reshape.25
  79.6 0.1 reshape.26
  79.7 12.4 %all_to_all.16 = f32[8,1,512]{2,1,0:T(1,128)S(1)} all-to-all(f32[8,1,512]{2,1,0:T(1,128)S(1)} %reshape.26), channel_id=1, replica_groups={{0,1,2,3,4,5,6,7},{8,9,10,11,12,13,14,15},{16,17,18,19,20,21,22,23},{24..., dimensions={0} | all-to-all | bytes 32768 | tf_op jit(solution)/shard_map/all_to_all | solution.py:280
  92.1 0.7 reduce.1
  92.8 0.1 reshape.27
  92.9 0.1 reshape.28
  93.0 17.8 %all_to_all.17 = f32[4,1,512]{2,1,0:T(1,128)S(1)} all-to-all(f32[4,1,512]{2,1,0:T(1,128)S(1)} %reshape.28), channel_id=1, replica_groups={{0,8,16,24},{1,9,17,25},{2,10,18,26},{3,11,19,27},{4,12,20,28},{5,13,21..., dimensions={0} | all-to-all | bytes 16384 | tf_op jit(solution)/shard_map/all_to_all | solution.py:280
  110.8 0.7 reduce.2
  111.5 0.1 reshape.29
  111.6 0.7 reshape.21
  (11 shorter events, 0.1 us)
Async XLA Ops:
  1.7 17.0 %collective-permute-start = (f32[9,2,64,128]{3,2,1,0:T(8,128)S(1)}, f32[9,2,64,128]{3,2,1,0:T(8,128)S(1)}, u32[]{:S(2)}, u32[]{:S(2)}) collective-permute-start(f32[9,2,64,128]{3,2,1,0:T(8,128)S(1)} %pad_maximum_fusion.own.s0), channel_id=1, source_target_pairs={{0,1},{1,2},{2,3},{3,4},{4,5},{5,6},{6,7},{7,8},{8,9},{9,10},{10,1... | collective-permute-start | bytes 1769480 | tf_op jit(solution)/shard_map/ppermute | solution.py:274
  5.1 16.7 %collective-permute-start.1 = (f32[9,2,64,128]{3,2,1,0:T(8,128)S(1)}, f32[9,2,64,128]{3,2,1,0:T(8,128)S(1)}, u32[]{:S(2)}, u32[]{:S(2)}) collective-permute-start(f32[9,2,64,128]{3,2,1,0:T(8,128)S(1)} %pad_maximum_fusion.own.s0), channel_id=1, source_target_pairs={{1,0},{2,1},{3,2},{4,3},{5,4},{6,5},{7,6},{8,7},{9,8},{10,9},{11,1... | collective-permute-start | bytes 1769480 | tf_op jit(solution)/shard_map/ppermute | solution.py:274
  10.9 0.7 copy-start.2
  10.9 0.7 copy-start.3
  11.7 10.1 %copy-start = (f32[2,64,128]{2,1,0:T(8,128)S(1)}, f32[2,64,128]{2,1,0:T(8,128)}, u32[]{:S(2)}) copy-start(f32[2,64,128]{2,1,0:T(8,128)} %perm.1) | copy-start | bytes 196612
  14.3 0.7 copy-start.4
  24.1 14.4 %collective-permute-start.2 = (f32[8,2,64,128]{3,2,1,0:T(8,128)S(1)}, f32[8,2,64,128]{3,2,1,0:T(8,128)S(1)}, u32[]{:S(2)}, u32[]{:S(2)}) collective-permute-start(f32[8,2,64,128]{3,2,1,0:T(8,128)S(1)} %get-tuple-element.11.own.s2), channel_id=1, source_target_pairs={{0,1},{1,2},{2,3},{3,4},{4,5},{5,6},{6,7},{7,8},{8,9},{9,10},{10,1... | collective-permute-start | bytes 1572872 | tf_op jit(solution)/shard_map/ppermute | solution.py:274
  27.7 16.2 %collective-permute-start.3 = (f32[8,2,64,128]{3,2,1,0:T(8,128)S(1)}, f32[8,2,64,128]{3,2,1,0:T(8,128)S(1)}, u32[]{:S(2)}, u32[]{:S(2)}) collective-permute-start(f32[8,2,64,128]{3,2,1,0:T(8,128)S(1)} %get-tuple-element.11.own.s2), channel_id=1, source_target_pairs={{1,0},{2,1},{3,2},{4,3},{5,4},{6,5},{7,6},{8,7},{9,8},{10,9},{11,1... | collective-permute-start | bytes 1572872 | tf_op jit(solution)/shard_map/ppermute | solution.py:274
  46.3 8.3 %collective-permute-start.4 = (f32[8,64,128]{2,1,0:T(8,128)S(1)}, f32[8,64,128]{2,1,0:T(8,128)S(1)}, u32[]{:S(2)}, u32[]{:S(2)}) collective-permute-start(f32[8,64,128]{2,1,0:T(8,128)S(1)} %get-tuple-element.13.s4b), channel_id=1, source_target_pairs={{0,1},{1,2},{2,3},{3,4},{4,5},{5,6},{6,7},{7,8},{8,9},{9,10},{10,1... | collective-permute-start | bytes 786440 | tf_op jit(solution)/shard_map/ppermute | solution.py:274
  49.9 8.7 %collective-permute-start.5 = (f32[8,64,128]{2,1,0:T(8,128)S(1)}, f32[8,64,128]{2,1,0:T(8,128)S(1)}, u32[]{:S(2)}, u32[]{:S(2)}) collective-permute-start(f32[8,64,128]{2,1,0:T(8,128)S(1)} %get-tuple-element.12.s4a), channel_id=1, source_target_pairs={{1,0},{2,1},{3,2},{4,3},{5,4},{6,5},{7,6},{8,7},{9,8},{10,9},{11,1... | collective-permute-start | bytes 786440 | tf_op jit(solution)/shard_map/ppermute | solution.py:274
  52.1 6.4 %copy-start.1 = (s32[2,64,128]{2,1,0:T(8,128)S(1)}, s32[2,64,128]{2,1,0:T(8,128)}, u32[]{:S(2)}) copy-start(s32[2,64,128]{2,1,0:T(8,128)} %labels.1) | copy-start | bytes 196612

commit v2 on v1

--- a/solution.py
+++ b/solution.py
@@ -132,7 +132,14 @@
     return kernel
 
 
-def gradient(fl, s0, t1, s2, low2, high2, t3, s4a, s4b, out, fz, fy, fb):
+def pieces(x):
+    first = x.astype(jnp.bfloat16)
+    rest = x - first.astype(F32)
+    second = rest.astype(jnp.bfloat16)
+    return first, second, (rest - second.astype(F32)).astype(jnp.bfloat16)
+
+
+def gradient(fl, s0, low0, high0, t1, s2, low2, high2, t3, s4a, s4b, perm, labels, bins, out, fz, fy, fb, half):
     wide, deep = out.shape[-2:]
 
     def plane(stage, f, c, j):
@@ -153,7 +160,7 @@
 
     for r in range(0, wide, ROWS):
         rows = pl.ds(r, ROWS)
-        x_low = x_mid = x_high = jnp.zeros((ROWS, deep), F32)
+        x_low = x_mid = x_high = half_low = half_high = jnp.zeros((ROWS, deep), F32)
         acc_z, acc_y, acc_b = [[jnp.zeros((ROWS, deep), F32)] * 2 for _ in range(3)]
         for n in range(STEPS):
             for c in range(4):
@@ -179,8 +186,16 @@
                 if 0 < n < STEPS - 1:
                     x_low = x_low + (load(1, -1) * weight - w[0]) * (load(0, -1) - u[0])
                     x_high = x_high + (load(1, 2) * weight - w[1]) * (load(0, 2) - u[1])
-        out[0, rows, :] = x_low + x_mid
-        out[1, rows, :] = x_high + x_mid
+                elif n == 0:
+                    half_low = half_low + w[0] * (u[0] - low0[c, 1, rows, :])
+                    half_high = half_high + w[1] * (u[1] - high0[c, 0, rows, :])
+                else:
+                    half_low = half_low + (w[0] - weight * low0[4 + c, 1, rows, :]) * u[0]
+                    half_high = half_high + (w[1] - weight * high0[4 + c, 0, rows, :]) * u[1]
+        out[0, rows, :] = x_low + x_mid + half_low
+        out[1, rows, :] = x_high + x_mid + half_high
+        half[0, rows, :] = half_low
+        half[1, rows, :] = half_high
         for j in range(2):
             fz[j, rows, :] = acc_z[j]
             fy[j, rows, :] = acc_y[j]
@@ -196,52 +211,42 @@
         total = total + jnp.where(row == 0, b, pltpu.roll(y, 1, 0))
         out[j] = total
 
-
-def final(fl, it, s0, low0, high0, s4a, s4b, low4, high4, part, perm, labels, conc, sens, bins, coef):
-    wide, deep = perm.shape[-2:]
+    def bin_rows(k, total):
+        rows = pl.ds(pl.multiple_of(k * 8, 8), 8)
+        cells = [(out[j, rows, :], perm[j, rows, :], labels[j, rows, :]) for j in range(2)]
+        for j, far, at in ((0, low0, 1), (1, high0, 0)):
+            cells.append((half[j, rows, :], far[8, at, rows, :], far[9, at, rows, :].astype(jnp.int32)))
+        left, right = [], []
+        for g, weight, label in cells:
+            value = g * weight * fl[NORM_AT]
+            coarse, fine = ((label >> 5) & 3) * 4 + (label >> 7), label & 31
+            for i in range(8):
+                hit = jnp.broadcast_to(coarse[i : i + 1], (16, deep)) == lax.broadcasted_iota(
+                    jnp.int32, (16, deep), 0
+                )
+                left.append(jnp.where(hit, jnp.broadcast_to(value[i : i + 1], (16, deep)), 0.0))
+                hit = jnp.broadcast_to(fine[i : i + 1], (32, deep)) == lax.broadcasted_iota(
+                    jnp.int32, (32, deep), 0
+                )
+                right.append(jnp.where(hit, 1.0, 0.0).astype(jnp.bfloat16))
+        return total + lax.dot_general(
+            jnp.concatenate(pieces(jnp.concatenate(left, axis=1)), axis=0),
+            jnp.concatenate(right, axis=1),
+            (((1,), (1,)), ((), ())),
+            preferred_element_type=F32,
+        )
+
+    total = lax.fori_loop(0, wide // 8, bin_rows, jnp.zeros((48, 32), F32))
+    total = total[0:16] + total[16:32] + total[32:48]
+    for k in range(4):
+        bins[:, 32 * k : 32 * k + 32] = total[4 * k : 4 * k + 4]
+
+
+def last_step(fl, it, low0, perm, high0, low4, s4a, s4b, high4, conc, sens, coef):
     face_weights([low0[8, 1], perm[0], perm[1], high0[8, 0]], coef)
-
-    def bin_rows(k, total):
-        r = pl.multiple_of(k * 8, 8)
-        rows = pl.ds(r, 8)
-        for j in range(2):
-            g = part[j, rows, :]
-            for c in range(4):
-                weight = fl[S_AT + c]
-                u4, l1 = (s4a, s4b)[j][c, rows, :], (s4a, s4b)[j][4 + c, rows, :]
-                far = (low4, high4)[j]
-                u0, l5 = s0[c, j, rows, :], s0[4 + c, j, rows, :]
-                far0, at = ((low0, 1), (high0, 0))[j]
-                g = g + weight * (
-                    (far[4 + c, rows, :] - l1) * (far0[c, at, rows, :] - u0)
-                    + (far0[4 + c, at, rows, :] - l5) * (far[c, rows, :] - u4)
-                )
-            value = g * perm[j, rows, :] * fl[NORM_AT]
-            label = labels[j, rows, :]
-            coarse, fine = label >> 5, label & 31
-            left, right = [], []
-            for i in range(8):
-                spread = jnp.broadcast_to(coarse[i : i + 1], (16, deep))
-                hit = spread == lax.broadcasted_iota(jnp.int32, (16, deep), 0)
-                left.append(jnp.where(hit, jnp.broadcast_to(value[i : i + 1], (16, deep)), 0.0))
-                spread = jnp.broadcast_to(fine[i : i + 1], (32, deep))
-                hit = spread == lax.broadcasted_iota(jnp.int32, (32, deep), 0)
-                right.append(hit.astype(F32))
-            total = total + lax.dot_general(
-                jnp.concatenate(left, axis=1),
-                jnp.concatenate(right, axis=1),
-                (((1,), (1,)), ((), ())),
-                precision=lax.Precision.HIGHEST,
-                preferred_element_type=F32,
-            )
-        return total
-
-    bins[...] = lax.fori_loop(0, wide // 8, bin_rows, jnp.zeros((16, 32), F32))
-
     for f, out in ((0, conc), (1, sens)):
         def source(c, j):
-            k = f * 4 + c
-            return (low4, s4a, s4b, high4)[j + 1], (k,)
+            return (low4, s4a, s4b, high4)[j + 1], (f * 4 + c,)
 
         def target(c, j):
             return out, (c, j)
@@ -313,7 +318,7 @@
     voxel = inject_voxel[0]
     it = jnp.stack([voxel // (wide * deep) - here * rows, voxel % (wide * deep), arrival[0]])
 
-    s0 = jnp.concatenate([initial[0], cotangent[0], permeability[None]], axis=0)
+    s0 = jnp.concatenate([initial[0], cotangent[0], permeability[None], labels.astype(F32)[None]], axis=0)
     low0, high0 = neighbours(s0, s0)
     slab, plane = (8, 2, wide, deep), (8, wide, deep)
     coef = (4, 7, wide, deep)
@@ -327,13 +332,13 @@
         [(8, 4, wide, deep), plane, plane], [coef], "steps_3_4", 20_000_000,
     )
     low4, high4 = neighbours(s4a, s4b)
-    part, = call(
-        gradient, [s0, t1, s2, low2, high2, t3, s4a, s4b], [fl],
-        [(2, wide, deep)], [(2, wide, deep)] * 3, "gradient", 10_000_000,
-    )
-    conc, sens, bins = call(
-        final, [s0, low0, high0, s4a, s4b, low4, high4, part, permeability, labels], [fl, it],
-        [(4, 2, wide, deep), (4, 2, wide, deep), (16, 32)], [(2, 7, wide, deep)], "final", 20_000_000,
+    bins, = call(
+        gradient, [s0, low0, high0, t1, s2, low2, high2, t3, s4a, s4b, permeability, labels], [fl],
+        [(4, 128)], [(2, wide, deep)] * 5, "gradient", 20_000_000,
+    )
+    conc, sens = call(
+        last_step, [low0, permeability, high0, low4, s4a, s4b, high4], [fl, it],
+        [(4, 2, wide, deep)] * 2, [(2, 7, wide, deep)], "step_5", 10_000_000,
     )
     bins = sum_over(bins, "exp", [list(range(exps))])
     near = 8 if spaces % 8 == 0 else spaces

time: 113 us -> 108 us (0.956)
  waiting for transfers between devices: 25.4 us -> 15.2 us
  blocking collectives: 44.9 us -> 52.1 us
  starting transfers between devices: 20.9 us -> 22.7 us
  local copies, waits for them, and re-layouts: 3.7 us -> 2 us
    ppermute x3, waiting for transfers between devices: 12.7 us -> 3.25 us  [neighbours(): lax.ppermute(block_high, 'space', forward)]
    all_to_all x3, blocking collectives: 44.9 us -> 52.1 us  [sum_over(): lax.all_to_all(copies, axis, 0, 0, axis_index_groups=groups, tiled=True)]
    all_to_all x3 -> x0, other arithmetic: 2.08 us -> none  [sum_over(): lax.all_to_all(copies, axis, 0, 0, axis_index_groups=groups, tiled=True)]
    ppermute x3, starting transfers between devices: 10.2 us -> 11.8 us  [neighbours(): lax.ppermute(block_low, 'space', backward)]
  transfers between devices with their start and end apart: 6 -> 6, of which waited for: 6 -> 4; matrix products, arithmetic and copies ran while one was open for 1% -> 1% of each run, Pallas kernels for 2% -> 4%
where the time goes in v2:
time: 108 us
  blocking collectives  52.1 us (48%)
  starting transfers between devices  22.7 us (21%)
  waiting for transfers between devices  15.2 us (14%)
  Pallas kernels  10.1 us (9%)
  other arithmetic  2.82 us (3%)
  between operations  2.74 us (3%)
  local copies, waits for them, and re-layouts  2 us (2%)
    all_to_all x3, blocking collectives, sum_over(): lax.all_to_all(copies, axis, 0, 0, axis_index_groups=groups, tiled=True)  52.1 us
    ppermute x3, waiting for transfers between devices, neighbours(): lax.ppermute(block_low, 'space', backward)  11.9 us
    ppermute x3, starting transfers between devices, neighbours(): lax.ppermute(block_low, 'space', backward)  11.8 us
    ppermute x3, starting transfers between devices, neighbours(): lax.ppermute(block_high, 'space', forward)  10.9 us
    pallas_call x4, Pallas kernels, call(): pl.pallas_call(kernel, out_shape=[jax.ShapeDtypeStruct(s, F32) for s in o...  10.1 us
    ppermute x3, waiting for transfers between devices, neighbours(): lax.ppermute(block_high, 'space', forward)  3.25 us
  transfers between devices with their start and end apart: 6, of which 4 were waited for; matrix products, arithmetic and copies ran while one was open for 1% of the time, Pallas kernels for 4%

profile of v2, /device:TPU:2, one launch (start us, length us, event | category | flops | bytes accessed | tf_op | source)
XLA Modules:
  0.0 107.6 jit_solution(4092019768103344086)
XLA Ops:
  0.6 0.0 copy-start
  0.6 0.9 convert_bitcast_fusion
  1.5 0.0 copy-done
  1.5 1.1 pad_maximum_fusion.own.s0
  2.6 7.8 %collective-permute-start.1 = (f32[10,2,64,128]{3,2,1,0:T(8,128)S(1)}, f32[10,2,64,128]{3,2,1,0:T(8,128)S(1)}, u32[]{:S(2)}, u32[]{:S(2)}) collective-permute-start(f32[10,2,64,128]{3,2,1,0:T(8,128)S(1)} %pad_maximum_fusion.own.s0), channel_id=1, source_target_pairs={{1,0},{2,1},{3,2},{4,3},{5,4},{6,5},{7,6},{8,7},{9,8},{10,9},{11,1... | collective-permute-start | bytes 1966088 | tf_op jit(solution)/shard_map/ppermute | solution.py:279
  10.4 1.9 %collective-permute-start = (f32[10,2,64,128]{3,2,1,0:T(8,128)S(1)}, f32[10,2,64,128]{3,2,1,0:T(8,128)S(1)}, u32[]{:S(2)}, u32[]{:S(2)}) collective-permute-start(f32[10,2,64,128]{3,2,1,0:T(8,128)S(1)} %pad_maximum_fusion.own.s0), channel_id=1, source_target_pairs={{0,1},{1,2},{2,3},{3,4},{4,5},{5,6},{6,7},{7,8},{8,9},{9,10},{10,1... | collective-permute-start | bytes 1966088 | tf_op jit(solution)/shard_map/ppermute | solution.py:279
  12.4 0.0 copy-start.2
  12.4 0.0 copy-start.3
  12.4 0.1 copy.23
  12.5 0.6 copy-done.2
  13.1 0.0 copy-done.3
  13.1 0.1 fusion.1
  13.2 0.1 copy.24
  15.3 0.1 copy.27
  15.4 0.1 reshape.20
  15.5 0.1 copy.25
  15.6 0.1 copy.26
  15.7 0.1 reshape.19
  15.7 0.0 copy-start.4
  15.7 0.7 copy-done.4
  16.4 0.1 concatenate.6.fl
  16.5 0.1 pad_add_fusion.it
  16.6 4.4 %collective-permute-done.1.high.phigh.high0 = f32[10,2,64,128]{3,2,1,0:T(8,128)S(1)} collective-permute-done((f32[10,2,64,128]{3,2,1,0:T(8,128)S(1)}, f32[10,2,64,128]{3,2,1,0:T(8,128)S(1)}, u32[]{:S(2)}, u32[]{:S(2)}) %collective-permute-start.1) | collective-permute-done | bytes 655392 | tf_op jit(solution)/shard_map/ppermute | solution.py:279
  21.0 1.9 %collective-permute-done.low.plow.low0 = f32[10,2,64,128]{3,2,1,0:T(8,128)S(1)} collective-permute-done((f32[10,2,64,128]{3,2,1,0:T(8,128)S(1)}, f32[10,2,64,128]{3,2,1,0:T(8,128)S(1)}, u32[]{:S(2)}, u32[]{:S(2)}) %collective-permute-start) | collective-permute-done | bytes 655392 | tf_op jit(solution)/shard_map/ppermute | solution.py:279
  22.9 2.2 %steps_1_2.1 = (f32[8,4,64,128]{3,2,1,0:T(8,128)S(1)}, f32[8,2,64,128]{3,2,1,0:T(8,128)S(1)}) custom-call(f32[44]{0:T(128)S(1)} %concatenate.6.fl, s32[3]{0:T(128)S(1)} %pad_add_fusion.it, f32[10,2,64,128]{3,2,1,0:T(8,128)S(1)} %pad_maximum_fusion.own.s0, f32[10,2,64,128]{3,2,1,0:T(8,128)S(1)} %collective-permute-done.low.plow.low0, ...), custom_call_target="tpu_custom_call" | custom-call | flops 20000000 | bytes 4915200 | tf_op jit(solution)/shard_map/steps_1_2/pallas_call | solution.py:263
  25.1 0.0 copy-start.1
  25.1 2.1 %collective-permute-start.3 = (f32[8,2,64,128]{3,2,1,0:T(8,128)S(1)}, f32[8,2,64,128]{3,2,1,0:T(8,128)S(1)}, u32[]{:S(2)}, u32[]{:S(2)}) collective-permute-start(f32[8,2,64,128]{3,2,1,0:T(8,128)S(1)} %get-tuple-element.10.own.s2), channel_id=1, source_target_pairs={{1,0},{2,1},{3,2},{4,3},{5,4},{6,5},{7,6},{8,7},{9,8},{10,9},{11,1... | collective-permute-start | bytes 1572872 | tf_op jit(solution)/shard_map/ppermute | solution.py:279
  27.2 3.9 %collective-permute-start.2 = (f32[8,2,64,128]{3,2,1,0:T(8,128)S(1)}, f32[8,2,64,128]{3,2,1,0:T(8,128)S(1)}, u32[]{:S(2)}, u32[]{:S(2)}) collective-permute-start(f32[8,2,64,128]{3,2,1,0:T(8,128)S(1)} %get-tuple-element.10.own.s2), channel_id=1, source_target_pairs={{0,1},{1,2},{2,3},{3,4},{4,5},{5,6},{6,7},{7,8},{8,9},{9,10},{10,1... | collective-permute-start | bytes 1572872 | tf_op jit(solution)/shard_map/ppermute | solution.py:279
  31.1 7.5 %collective-permute-done.3.high.high2 = f32[8,2,64,128]{3,2,1,0:T(8,128)S(1)} collective-permute-done((f32[8,2,64,128]{3,2,1,0:T(8,128)S(1)}, f32[8,2,64,128]{3,2,1,0:T(8,128)S(1)}, u32[]{:S(2)}, u32[]{:S(2)}) %collective-permute-start.3) | collective-permute-done | bytes 524320 | tf_op jit(solution)/shard_map/ppermute | solution.py:279
  38.6 1.3 %collective-permute-done.2.low.low2 = f32[8,2,64,128]{3,2,1,0:T(8,128)S(1)} collective-permute-done((f32[8,2,64,128]{3,2,1,0:T(8,128)S(1)}, f32[8,2,64,128]{3,2,1,0:T(8,128)S(1)}, u32[]{:S(2)}, u32[]{:S(2)}) %collective-permute-start.2) | collective-permute-done | bytes 524320 | tf_op jit(solution)/shard_map/ppermute | solution.py:279
  39.9 2.3 %steps_3_4.1 = (f32[8,4,64,128]{3,2,1,0:T(8,128)S(1)}, f32[8,64,128]{2,1,0:T(8,128)S(1)}, f32[8,64,128]{2,1,0:T(8,128)S(1)}) custom-call(f32[44]{0:T(128)S(1)} %concatenate.6.fl, s32[3]{0:T(128)S(1)} %pad_add_fusion.it, f32[8,2,64,128]{3,2,1,0:T(8,128)S(1)} %get-tuple-element.10.own.s2, f32[8,2,64,128]{3,2,1,0:T(8,128)S(1)} %collective-permute-done.2.low.low2, ...), custom_call_target="tpu_custom_call" | custom-call | flops 20000000 | bytes 4521984 | tf_op jit(solution)/shard_map/steps_3_4/pallas_call | solution.py:263
  42.2 5.1 %collective-permute-start.4 = (f32[8,64,128]{2,1,0:T(8,128)S(1)}, f32[8,64,128]{2,1,0:T(8,128)S(1)}, u32[]{:S(2)}, u32[]{:S(2)}) collective-permute-start(f32[8,64,128]{2,1,0:T(8,128)S(1)} %get-tuple-element.11.s4b), channel_id=1, source_target_pairs={{0,1},{1,2},{2,3},{3,4},{4,5},{5,6},{6,7},{7,8},{8,9},{9,10},{10,1... | collective-permute-start | bytes 786440 | tf_op jit(solution)/shard_map/ppermute | solution.py:279
  47.3 1.9 %collective-permute-start.5 = (f32[8,64,128]{2,1,0:T(8,128)S(1)}, f32[8,64,128]{2,1,0:T(8,128)S(1)}, u32[]{:S(2)}, u32[]{:S(2)}) collective-permute-start(f32[8,64,128]{2,1,0:T(8,128)S(1)} %get-tuple-element.12.s4a), channel_id=1, source_target_pairs={{1,0},{2,1},{3,2},{4,3},{5,4},{6,5},{7,6},{8,7},{9,8},{10,9},{11,1... | collective-permute-start | bytes 786440 | tf_op jit(solution)/shard_map/ppermute | solution.py:279
  49.3 0.0 copy-done.1
  49.3 3.8 %gradient.1 = f32[4,128]{1,0:T(4,128)S(1)} custom-call(f32[44]{0:T(128)S(1)} %concatenate.6.fl, f32[10,2,64,128]{3,2,1,0:T(8,128)S(1)} %pad_maximum_fusion.own.s0, f32[10,2,64,128]{3,2,1,0:T(8,128)S(1)} %collective-permute-done.low.plow.low0, f32[10,2,64,128]{3,2,1,0:T(8,128)S(1)} %collective-permute-done.1.high.phigh.high0, ...), custom_call_target="tpu_custom_call" | custom-call | flops 20000000 | bytes 6293504 | tf_op jit(solution)/shard_map/gradient/pallas_call | solution.py:263
  53.1 15.4 %all_to_all.15 = f32[16,4,128]{2,1,0:T(4,128)S(1)} all-to-all(f32[16,4,128]{2,1,0:T(4,128)S(1)} %broadcast_in_dim.54), channel_id=1, replica_groups={{0,32,64,96,128,160,192,224,256,288,320,352,384,416,448,480},{1,33,65,9..., dimensions={0} | all-to-all | bytes 65536 | tf_op jit(solution)/shard_map/all_to_all | solution.py:285
  68.5 16.7 %all_to_all.16 = f32[8,4,128]{2,1,0:T(4,128)S(1)} all-to-all(f32[8,4,128]{2,1,0:T(4,128)S(1)} %broadcast_in_dim.55), channel_id=1, replica_groups={{0,1,2,3,4,5,6,7},{8,9,10,11,12,13,14,15},{16,17,18,19,20,21,22,23},{24..., dimensions={0} | all-to-all | bytes 32768 | tf_op jit(solution)/shard_map/all_to_all | solution.py:285
  85.2 20.0 %all_to_all.17 = f32[4,4,128]{2,1,0:T(4,128)S(1)} all-to-all(f32[4,4,128]{2,1,0:T(4,128)S(1)} %broadcast_in_dim.56), channel_id=1, replica_groups={{0,8,16,24},{1,9,17,25},{2,10,18,26},{3,11,19,27},{4,12,20,28},{5,13,21..., dimensions={0} | all-to-all | bytes 16384 | tf_op jit(solution)/shard_map/all_to_all | solution.py:285
  105.2 0.6 reduce_sum.39
  105.8 0.0 collective-permute-done.4.low4
  105.8 0.0 collective-permute-done.5.high4
  105.8 1.8 %step_5.1 = (f32[4,2,64,128]{3,2,1,0:T(8,128)}, f32[4,2,64,128]{3,2,1,0:T(8,128)}) custom-call(f32[44]{0:T(128)S(1)} %concatenate.6.fl, s32[3]{0:T(128)S(1)} %pad_add_fusion.it, f32[10,2,64,128]{3,2,1,0:T(8,128)S(1)} %collective-permute-done.low.plow.low0, f32[2,64,128]{2,1,0:T(8,128)S(1)} %copy-done, ...), custom_call_target="tpu_custom_call" | custom-call | flops 10000000 | bytes 2949120 | tf_op jit(solution)/shard_map/step_5/pallas_call | solution.py:263
  (10 shorter events, 0.1 us)
Async XLA Ops:
  0.6 0.9 copy-start
  2.6 18.4 %collective-permute-start.1 = (f32[10,2,64,128]{3,2,1,0:T(8,128)S(1)}, f32[10,2,64,128]{3,2,1,0:T(8,128)S(1)}, u32[]{:S(2)}, u32[]{:S(2)}) collective-permute-start(f32[10,2,64,128]{3,2,1,0:T(8,128)S(1)} %pad_maximum_fusion.own.s0), channel_id=1, source_target_pairs={{1,0},{2,1},{3,2},{4,3},{5,4},{6,5},{7,6},{8,7},{9,8},{10,9},{11,1... | collective-permute-start | bytes 1966088 | tf_op jit(solution)/shard_map/ppermute | solution.py:279
  10.4 12.5 %collective-permute-start = (f32[10,2,64,128]{3,2,1,0:T(8,128)S(1)}, f32[10,2,64,128]{3,2,1,0:T(8,128)S(1)}, u32[]{:S(2)}, u32[]{:S(2)}) collective-permute-start(f32[10,2,64,128]{3,2,1,0:T(8,128)S(1)} %pad_maximum_fusion.own.s0), channel_id=1, source_target_pairs={{0,1},{1,2},{2,3},{3,4},{4,5},{5,6},{6,7},{7,8},{8,9},{9,10},{10,1... | collective-permute-start | bytes 1966088 | tf_op jit(solution)/shard_map/ppermute | solution.py:279
  12.4 0.7 copy-start.2
  12.4 0.7 copy-start.3
  15.7 0.7 copy-start.4
  25.1 24.2 %copy-start.1 = (s32[2,64,128]{2,1,0:T(8,128)S(1)}, s32[2,64,128]{2,1,0:T(8,128)}, u32[]{:S(2)}) copy-start(s32[2,64,128]{2,1,0:T(8,128)} %labels.1) | copy-start | bytes 196612
  25.1 13.5 %collective-permute-start.3 = (f32[8,2,64,128]{3,2,1,0:T(8,128)S(1)}, f32[8,2,64,128]{3,2,1,0:T(8,128)S(1)}, u32[]{:S(2)}, u32[]{:S(2)}) collective-permute-start(f32[8,2,64,128]{3,2,1,0:T(8,128)S(1)} %get-tuple-element.10.own.s2), channel_id=1, source_target_pairs={{1,0},{2,1},{3,2},{4,3},{5,4},{6,5},{7,6},{8,7},{9,8},{10,9},{11,1... | collective-permute-start | bytes 1572872 | tf_op jit(solution)/shard_map/ppermute | solution.py:279
  27.2 12.8 %collective-permute-start.2 = (f32[8,2,64,128]{3,2,1,0:T(8,128)S(1)}, f32[8,2,64,128]{3,2,1,0:T(8,128)S(1)}, u32[]{:S(2)}, u32[]{:S(2)}) collective-permute-start(f32[8,2,64,128]{3,2,1,0:T(8,128)S(1)} %get-tuple-element.10.own.s2), channel_id=1, source_target_pairs={{0,1},{1,2},{2,3},{3,4},{4,5},{5,6},{6,7},{7,8},{8,9},{9,10},{10,1... | collective-permute-start | bytes 1572872 | tf_op jit(solution)/shard_map/ppermute | solution.py:279
  42.2 63.6 %collective-permute-start.4 = (f32[8,64,128]{2,1,0:T(8,128)S(1)}, f32[8,64,128]{2,1,0:T(8,128)S(1)}, u32[]{:S(2)}, u32[]{:S(2)}) collective-permute-start(f32[8,64,128]{2,1,0:T(8,128)S(1)} %get-tuple-element.11.s4b), channel_id=1, source_target_pairs={{0,1},{1,2},{2,3},{3,4},{4,5},{5,6},{6,7},{7,8},{8,9},{9,10},{10,1... | collective-permute-start | bytes 786440 | tf_op jit(solution)/shard_map/ppermute | solution.py:279
  47.3 58.5 %collective-permute-start.5 = (f32[8,64,128]{2,1,0:T(8,128)S(1)}, f32[8,64,128]{2,1,0:T(8,128)S(1)}, u32[]{:S(2)}, u32[]{:S(2)}) collective-permute-start(f32[8,64,128]{2,1,0:T(8,128)S(1)} %get-tuple-element.12.s4a), channel_id=1, source_target_pairs={{1,0},{2,1},{3,2},{4,3},{5,4},{6,5},{7,6},{8,7},{9,8},{10,9},{11,1... | collective-permute-start | bytes 786440 | tf_op jit(solution)/shard_map/ppermute | solution.py:279

commit v3 on v2

--- a/solution.py
+++ b/solution.py
@@ -100,8 +100,11 @@
 
 
 def two_steps(first_step, perm_at):
-    def kernel(fl, it, own, low, high, plow, pmid, phigh, mid, *rest):
-        out, coef = rest[:-1], rest[-1]
+    def kernel(fl, it, own, low, high, plow, pmid, phigh, *rest):
+        labels, rest = (rest[:1], rest[1:]) if first_step == 0 else ((), rest)
+        mid, out, coef = rest[0], rest[1:-1], rest[-1]
+        for ref in labels:
+            out[0][8] = ref[...].astype(F32)
         planes = [plow[(*perm_at, 0)], plow[(*perm_at, 1)], pmid[0], pmid[1]]
         planes += [phigh[(*perm_at, 0)], phigh[(*perm_at, 1)]]
         face_weights(planes, coef)
@@ -214,8 +217,8 @@
     def bin_rows(k, total):
         rows = pl.ds(pl.multiple_of(k * 8, 8), 8)
         cells = [(out[j, rows, :], perm[j, rows, :], labels[j, rows, :]) for j in range(2)]
-        for j, far, at in ((0, low0, 1), (1, high0, 0)):
-            cells.append((half[j, rows, :], far[8, at, rows, :], far[9, at, rows, :].astype(jnp.int32)))
+        for j, far, names, at in ((0, low0, low2, 1), (1, high0, high2, 0)):
+            cells.append((half[j, rows, :], far[8, at, rows, :], names[8, at, rows, :].astype(jnp.int32)))
         left, right = [], []
         for g, weight, label in cells:
             value = g * weight * fl[NORM_AT]
@@ -318,33 +321,34 @@
     voxel = inject_voxel[0]
     it = jnp.stack([voxel // (wide * deep) - here * rows, voxel % (wide * deep), arrival[0]])
 
-    s0 = jnp.concatenate([initial[0], cotangent[0], permeability[None], labels.astype(F32)[None]], axis=0)
+    s0 = jnp.concatenate([initial[0], cotangent[0], permeability[None]], axis=0)
     low0, high0 = neighbours(s0, s0)
-    slab, plane = (8, 2, wide, deep), (8, wide, deep)
+    plane = (8, wide, deep)
     coef = (4, 7, wide, deep)
     t1, s2 = call(
-        two_steps(0, (8,)), [s0, low0, high0, low0, permeability, high0], [fl, it],
-        [(8, 4, wide, deep), slab], [coef], "steps_1_2", 20_000_000,
+        two_steps(0, (8,)), [s0, low0, high0, low0, permeability, high0, labels], [fl, it],
+        [(8, 4, wide, deep), (9, 2, wide, deep)], [coef], "steps_1_2", 20_000_000,
     )
     low2, high2 = neighbours(s2, s2)
     t3, s4a, s4b = call(
         two_steps(2, (8,)), [s2, low2, high2, low0, permeability, high0], [fl, it],
         [(8, 4, wide, deep), plane, plane], [coef], "steps_3_4", 20_000_000,
     )
-    low4, high4 = neighbours(s4a, s4b)
     bins, = call(
         gradient, [s0, low0, high0, t1, s2, low2, high2, t3, s4a, s4b, permeability, labels], [fl],
         [(4, 128)], [(2, wide, deep)] * 5, "gradient", 20_000_000,
     )
+    near = 4 if spaces % 4 == 0 else spaces
+    bins = sum_over(bins, "space", [[g * near + i for i in range(near)] for g in range(spaces // near)])
+    if spaces > near:
+        bins = sum_over(bins, "space", [[g * near + i for g in range(spaces // near)] for i in range(near)])
+    bins, last_low, last_high = lax.optimization_barrier((bins, s4a, s4b))
+    low4, high4 = neighbours(last_low, last_high)
     conc, sens = call(
         last_step, [low0, permeability, high0, low4, s4a, s4b, high4], [fl, it],
         [(4, 2, wide, deep)] * 2, [(2, 7, wide, deep)], "step_5", 10_000_000,
     )
     bins = sum_over(bins, "exp", [list(range(exps))])
-    near = 8 if spaces % 8 == 0 else spaces
-    bins = sum_over(bins, "space", [[g * near + i for i in range(near)] for g in range(spaces // near)])
-    if spaces > near:
-        bins = sum_over(bins, "space", [[g * near + i for g in range(spaces // near)] for i in range(near)])
     return conc[None], sens[None], bins.reshape(-1)
 
 

time: 108 us -> 104 us (0.963)
  the two profiles are of different devices: /device:TPU:2 before, /device:TPU:65 now
where the time goes in v3:
time: 104 us
  blocking collectives  43.8 us (42%)
  waiting for transfers between devices  26 us (25%)
  starting transfers between devices  18.1 us (17%)
  Pallas kernels  10.1 us (10%)
  between operations  2.73 us (3%)
  other arithmetic  1.97 us (2%)
  local copies, waits for them, and re-layouts  1.34 us (1%)
    all_to_all x3, blocking collectives, sum_over(): lax.all_to_all(copies, axis, 0, 0, axis_index_groups=groups, tiled=True)  43.8 us
    ppermute x3, waiting for transfers between devices, neighbours(): lax.ppermute(block_low, 'space', backward)  16.7 us
    ppermute x3, starting transfers between devices, neighbours(): lax.ppermute(block_low, 'space', backward)  10.6 us
    pallas_call x4, Pallas kernels, call(): pl.pallas_call(kernel, out_shape=[jax.ShapeDtypeStruct(s, F32) for s in o...  10.1 us
    ppermute x3, waiting for transfers between devices, neighbours(): lax.ppermute(block_high, 'space', forward)  9.32 us
    ppermute x3, starting transfers between devices, neighbours(): lax.ppermute(block_high, 'space', forward)  7.47 us
  transfers between devices with their start and end apart: 6, of which 4 were waited for; matrix products, arithmetic and copies ran while one was open for 1% of the time, Pallas kernels for 0%

profile of v3, /device:TPU:65, one launch (start us, length us, event | category | flops | bytes accessed | tf_op | source)
XLA Modules:
  0.0 104.0 jit_solution(5124303180102272630)
XLA Ops:
  0.6 1.1 %pad_maximum_fusion.own.s0 = f32[9,2,64,128]{3,2,1,0:T(8,128)S(1)} fusion(f32[1,2,64,128]{3,2,1,0:T(8,128)} %bitcast.17, f32[4,2,64,128]{3,2,1,0:T(8,128)} %bitcast.18, f32[4,2,64,128]{3,2,1,0:T(8,128)} %bitcast.19), kind=kLoop, calls=%fused_computation | loop fusion | flops 294912 | bytes 1179648 | tf_op jit(solution)/shard_map/concatenate | solution.py:324
  1.7 3.5 %collective-permute-start.1 = (f32[9,2,64,128]{3,2,1,0:T(8,128)S(1)}, f32[9,2,64,128]{3,2,1,0:T(8,128)S(1)}, u32[]{:S(2)}, u32[]{:S(2)}) collective-permute-start(f32[9,2,64,128]{3,2,1,0:T(8,128)S(1)} %pad_maximum_fusion.own.s0), channel_id=1, source_target_pairs={{1,0},{2,1},{3,2},{4,3},{5,4},{6,5},{7,6},{8,7},{9,8},{10,9},{11,1... | collective-permute-start | bytes 1769480 | tf_op jit(solution)/shard_map/ppermute | solution.py:282
  5.2 1.9 %collective-permute-start = (f32[9,2,64,128]{3,2,1,0:T(8,128)S(1)}, f32[9,2,64,128]{3,2,1,0:T(8,128)S(1)}, u32[]{:S(2)}, u32[]{:S(2)}) collective-permute-start(f32[9,2,64,128]{3,2,1,0:T(8,128)S(1)} %pad_maximum_fusion.own.s0), channel_id=1, source_target_pairs={{0,1},{1,2},{2,3},{3,4},{4,5},{5,6},{6,7},{7,8},{8,9},{9,10},{10,1... | collective-permute-start | bytes 1769480 | tf_op jit(solution)/shard_map/ppermute | solution.py:282
  7.2 0.0 copy-start.2
  7.2 0.0 copy-start.3
  7.2 0.1 copy.23
  7.3 0.6 copy-done.2
  7.9 0.0 copy-done.3
  7.9 0.0 copy-start.4
  7.9 0.0 copy-start.1
  7.9 0.1 fusion.1
  8.0 0.0 copy-start
  8.0 0.1 copy.24
  10.1 0.1 copy.27
  10.2 0.1 reshape.20
  10.3 0.1 copy.25
  10.4 0.1 copy.26
  10.5 0.1 reshape.19
  10.6 0.0 copy-done.4
  10.6 0.1 concatenate.6.fl
  10.6 0.1 pad_add_fusion.it
  10.7 7.1 %collective-permute-done.1.high.phigh.high0 = f32[9,2,64,128]{3,2,1,0:T(8,128)S(1)} collective-permute-done((f32[9,2,64,128]{3,2,1,0:T(8,128)S(1)}, f32[9,2,64,128]{3,2,1,0:T(8,128)S(1)}, u32[]{:S(2)}, u32[]{:S(2)}) %collective-permute-start.1) | collective-permute-done | bytes 589856 | tf_op jit(solution)/shard_map/ppermute | solution.py:282
  17.8 5.3 %collective-permute-done.low.plow.low0 = f32[9,2,64,128]{3,2,1,0:T(8,128)S(1)} collective-permute-done((f32[9,2,64,128]{3,2,1,0:T(8,128)S(1)}, f32[9,2,64,128]{3,2,1,0:T(8,128)S(1)}, u32[]{:S(2)}, u32[]{:S(2)}) %collective-permute-start) | collective-permute-done | bytes 589856 | tf_op jit(solution)/shard_map/ppermute | solution.py:282
  23.1 0.0 copy-done.1
  23.1 0.0 copy-done
  23.1 2.2 %steps_1_2.1 = (f32[8,4,64,128]{3,2,1,0:T(8,128)S(1)}, f32[9,2,64,128]{3,2,1,0:T(8,128)S(1)}) custom-call(f32[44]{0:T(128)S(1)} %concatenate.6.fl, s32[3]{0:T(128)S(1)} %pad_add_fusion.it, f32[9,2,64,128]{3,2,1,0:T(8,128)S(1)} %pad_maximum_fusion.own.s0, f32[9,2,64,128]{3,2,1,0:T(8,128)S(1)} %collective-permute-done.low.plow.low0, ...), custom_call_target="tpu_custom_call" | custom-call | flops 20000000 | bytes 4718592 | tf_op jit(solution)/shard_map/steps_1_2/pallas_call | solution.py:266
  25.3 1.9 %collective-permute-start.3 = (f32[9,2,64,128]{3,2,1,0:T(8,128)S(1)}, f32[9,2,64,128]{3,2,1,0:T(8,128)S(1)}, u32[]{:S(2)}, u32[]{:S(2)}) collective-permute-start(f32[9,2,64,128]{3,2,1,0:T(8,128)S(1)} %get-tuple-element.14.own.s2), channel_id=1, source_target_pairs={{1,0},{2,1},{3,2},{4,3},{5,4},{6,5},{7,6},{8,7},{9,8},{10,9},{11,1... | collective-permute-start | bytes 1769480 | tf_op jit(solution)/shard_map/ppermute | solution.py:282
  27.2 3.4 %collective-permute-start.2 = (f32[9,2,64,128]{3,2,1,0:T(8,128)S(1)}, f32[9,2,64,128]{3,2,1,0:T(8,128)S(1)}, u32[]{:S(2)}, u32[]{:S(2)}) collective-permute-start(f32[9,2,64,128]{3,2,1,0:T(8,128)S(1)} %get-tuple-element.14.own.s2), channel_id=1, source_target_pairs={{0,1},{1,2},{2,3},{3,4},{4,5},{5,6},{6,7},{7,8},{8,9},{9,10},{10,1... | collective-permute-start | bytes 1769480 | tf_op jit(solution)/shard_map/ppermute | solution.py:282
  30.6 9.6 %collective-permute-done.3.high.high2 = f32[9,2,64,128]{3,2,1,0:T(8,128)S(1)} collective-permute-done((f32[9,2,64,128]{3,2,1,0:T(8,128)S(1)}, f32[9,2,64,128]{3,2,1,0:T(8,128)S(1)}, u32[]{:S(2)}, u32[]{:S(2)}) %collective-permute-start.3) | collective-permute-done | bytes 589856 | tf_op jit(solution)/shard_map/ppermute | solution.py:282
  40.2 4.0 %collective-permute-done.2.low.low2 = f32[9,2,64,128]{3,2,1,0:T(8,128)S(1)} collective-permute-done((f32[9,2,64,128]{3,2,1,0:T(8,128)S(1)}, f32[9,2,64,128]{3,2,1,0:T(8,128)S(1)}, u32[]{:S(2)}, u32[]{:S(2)}) %collective-permute-start.2) | collective-permute-done | bytes 589856 | tf_op jit(solution)/shard_map/ppermute | solution.py:282
  44.2 2.3 %steps_3_4.1 = (f32[8,4,64,128]{3,2,1,0:T(8,128)S(1)}, f32[8,64,128]{2,1,0:T(8,128)S(1)}, f32[8,64,128]{2,1,0:T(8,128)S(1)}) custom-call(f32[44]{0:T(128)S(1)} %concatenate.6.fl, s32[3]{0:T(128)S(1)} %pad_add_fusion.it, f32[9,2,64,128]{3,2,1,0:T(8,128)S(1)} %get-tuple-element.14.own.s2, f32[9,2,64,128]{3,2,1,0:T(8,128)S(1)} %collective-permute-done.2.low.low2, ...), custom_call_target="tpu_custom_call" | custom-call | flops 20000000 | bytes 4587520 | tf_op jit(solution)/shard_map/steps_3_4/pallas_call | solution.py:266
  46.5 3.8 %gradient.1 = f32[4,128]{1,0:T(4,128)S(1)} custom-call(f32[44]{0:T(128)S(1)} %concatenate.6.fl, f32[9,2,64,128]{3,2,1,0:T(8,128)S(1)} %pad_maximum_fusion.own.s0, f32[9,2,64,128]{3,2,1,0:T(8,128)S(1)} %collective-permute-done.low.plow.low0, f32[9,2,64,128]{3,2,1,0:T(8,128)S(1)} %collective-permute-done.1.high.phigh.high0, ...), custom_call_target="tpu_custom_call" | custom-call | flops 20000000 | bytes 6293504 | tf_op jit(solution)/shard_map/gradient/pallas_call | solution.py:266
  50.3 6.5 %all_to_all.15 = f32[4,4,128]{2,1,0:T(4,128)S(1)} all-to-all(f32[4,4,128]{2,1,0:T(4,128)S(1)} %broadcast_in_dim.48), channel_id=1, replica_groups={{0,1,2,3},{4,5,6,7},{8,9,10,11},{12,13,14,15},{16,17,18,19},{20,21,22,2..., dimensions={0} | all-to-all | bytes 16384 | tf_op jit(solution)/shard_map/all_to_all | solution.py:288
  56.8 17.1 %all_to_all.16 = f32[8,4,128]{2,1,0:T(4,128)S(1)} all-to-all(f32[8,4,128]{2,1,0:T(4,128)S(1)} %broadcast_in_dim.49), channel_id=1, replica_groups={{0,4,8,12,16,20,24,28},{1,5,9,13,17,21,25,29},{2,6,10,14,18,22,26,30},{..., dimensions={0} | all-to-all | bytes 32768 | tf_op jit(solution)/shard_map/all_to_all | solution.py:288
  73.9 2.2 %collective-permute-start.4 = (f32[8,64,128]{2,1,0:T(8,128)S(1)}, f32[8,64,128]{2,1,0:T(8,128)S(1)}, u32[]{:S(2)}, u32[]{:S(2)}) collective-permute-start(f32[8,64,128]{2,1,0:T(8,128)S(1)} %get-tuple-element.18.s4b), channel_id=1, source_target_pairs={{0,1},{1,2},{2,3},{3,4},{4,5},{5,6},{6,7},{7,8},{8,9},{9,10},{10,1... | collective-permute-start | bytes 786440 | tf_op jit(solution)/shard_map/ppermute | solution.py:282
  76.1 5.2 %collective-permute-start.5 = (f32[8,64,128]{2,1,0:T(8,128)S(1)}, f32[8,64,128]{2,1,0:T(8,128)S(1)}, u32[]{:S(2)}, u32[]{:S(2)}) collective-permute-start(f32[8,64,128]{2,1,0:T(8,128)S(1)} %get-tuple-element.19.s4a), channel_id=1, source_target_pairs={{1,0},{2,1},{3,2},{4,3},{5,4},{6,5},{7,6},{8,7},{9,8},{10,9},{11,1... | collective-permute-start | bytes 786440 | tf_op jit(solution)/shard_map/ppermute | solution.py:282
  81.3 20.2 %all_to_all.17 = f32[16,4,128]{2,1,0:T(4,128)S(1)} all-to-all(f32[16,4,128]{2,1,0:T(4,128)S(1)} %broadcast_in_dim.52), channel_id=1, replica_groups={{0,32,64,96,128,160,192,224,256,288,320,352,384,416,448,480},{1,33,65,9..., dimensions={0} | all-to-all | bytes 65536 | tf_op jit(solution)/shard_map/all_to_all | solution.py:288
  101.6 0.6 reduce_sum.39
  102.2 0.0 collective-permute-done.4.low4
  102.2 0.0 collective-permute-done.5.high4
  102.2 1.8 %step_5.1 = (f32[4,2,64,128]{3,2,1,0:T(8,128)}, f32[4,2,64,128]{3,2,1,0:T(8,128)}) custom-call(f32[44]{0:T(128)S(1)} %concatenate.6.fl, s32[3]{0:T(128)S(1)} %pad_add_fusion.it, f32[9,2,64,128]{3,2,1,0:T(8,128)S(1)} %collective-permute-done.low.plow.low0, f32[2,64,128]{2,1,0:T(8,128)S(1)} %copy-done, ...), custom_call_target="tpu_custom_call" | custom-call | flops 10000000 | bytes 2818048 | tf_op jit(solution)/shard_map/step_5/pallas_call | solution.py:266
  (10 shorter events, 0.1 us)
Async XLA Ops:
  1.7 16.1 %collective-permute-start.1 = (f32[9,2,64,128]{3,2,1,0:T(8,128)S(1)}, f32[9,2,64,128]{3,2,1,0:T(8,128)S(1)}, u32[]{:S(2)}, u32[]{:S(2)}) collective-permute-start(f32[9,2,64,128]{3,2,1,0:T(8,128)S(1)} %pad_maximum_fusion.own.s0), channel_id=1, source_target_pairs={{1,0},{2,1},{3,2},{4,3},{5,4},{6,5},{7,6},{8,7},{9,8},{10,9},{11,1... | collective-permute-start | bytes 1769480 | tf_op jit(solution)/shard_map/ppermute | solution.py:282
  5.2 17.9 %collective-permute-start = (f32[9,2,64,128]{3,2,1,0:T(8,128)S(1)}, f32[9,2,64,128]{3,2,1,0:T(8,128)S(1)}, u32[]{:S(2)}, u32[]{:S(2)}) collective-permute-start(f32[9,2,64,128]{3,2,1,0:T(8,128)S(1)} %pad_maximum_fusion.own.s0), channel_id=1, source_target_pairs={{0,1},{1,2},{2,3},{3,4},{4,5},{5,6},{6,7},{7,8},{8,9},{9,10},{10,1... | collective-permute-start | bytes 1769480 | tf_op jit(solution)/shard_map/ppermute | solution.py:282
  7.2 0.7 copy-start.2
  7.2 0.7 copy-start.3
  7.9 2.7 %copy-start.4 = (f32[4]{0:T(128)S(1)}, f32[4]{0:T(128)}, u32[]{:S(2)}) copy-start(f32[4]{0:T(128)} %param.14) | copy-start | bytes 52
  7.9 15.2 %copy-start.1 = (s32[2,64,128]{2,1,0:T(8,128)S(1)}, s32[2,64,128]{2,1,0:T(8,128)}, u32[]{:S(2)}) copy-start(s32[2,64,128]{2,1,0:T(8,128)} %labels.1) | copy-start | bytes 196612
  8.0 15.1 %copy-start = (f32[2,64,128]{2,1,0:T(8,128)S(1)}, f32[2,64,128]{2,1,0:T(8,128)}, u32[]{:S(2)}) copy-start(f32[2,64,128]{2,1,0:T(8,128)} %perm.3) | copy-start | bytes 196612
  25.3 14.9 %collective-permute-start.3 = (f32[9,2,64,128]{3,2,1,0:T(8,128)S(1)}, f32[9,2,64,128]{3,2,1,0:T(8,128)S(1)}, u32[]{:S(2)}, u32[]{:S(2)}) collective-permute-start(f32[9,2,64,128]{3,2,1,0:T(8,128)S(1)} %get-tuple-element.14.own.s2), channel_id=1, source_target_pairs={{1,0},{2,1},{3,2},{4,3},{5,4},{6,5},{7,6},{8,7},{9,8},{10,9},{11,1... | collective-permute-start | bytes 1769480 | tf_op jit(solution)/shard_map/ppermute | solution.py:282
  27.2 17.0 %collective-permute-start.2 = (f32[9,2,64,128]{3,2,1,0:T(8,128)S(1)}, f32[9,2,64,128]{3,2,1,0:T(8,128)S(1)}, u32[]{:S(2)}, u32[]{:S(2)}) collective-permute-start(f32[9,2,64,128]{3,2,1,0:T(8,128)S(1)} %get-tuple-element.14.own.s2), channel_id=1, source_target_pairs={{0,1},{1,2},{2,3},{3,4},{4,5},{5,6},{6,7},{7,8},{8,9},{9,10},{10,1... | collective-permute-start | bytes 1769480 | tf_op jit(solution)/shard_map/ppermute | solution.py:282
  73.9 28.2 %collective-permute-start.4 = (f32[8,64,128]{2,1,0:T(8,128)S(1)}, f32[8,64,128]{2,1,0:T(8,128)S(1)}, u32[]{:S(2)}, u32[]{:S(2)}) collective-permute-start(f32[8,64,128]{2,1,0:T(8,128)S(1)} %get-tuple-element.18.s4b), channel_id=1, source_target_pairs={{0,1},{1,2},{2,3},{3,4},{4,5},{5,6},{6,7},{7,8},{8,9},{9,10},{10,1... | collective-permute-start | bytes 786440 | tf_op jit(solution)/shard_map/ppermute | solution.py:282
  76.1 26.1 %collective-permute-start.5 = (f32[8,64,128]{2,1,0:T(8,128)S(1)}, f32[8,64,128]{2,1,0:T(8,128)S(1)}, u32[]{:S(2)}, u32[]{:S(2)}) collective-permute-start(f32[8,64,128]{2,1,0:T(8,128)S(1)} %get-tuple-element.19.s4a), channel_id=1, source_target_pairs={{1,0},{2,1},{3,2},{4,3},{5,4},{6,5},{7,6},{8,7},{9,8},{10,9},{11,1... | collective-permute-start | bytes 786440 | tf_op jit(solution)/shard_map/ppermute | solution.py:282

commit v4 on v3

--- a/solution.py
+++ b/solution.py
@@ -95,8 +95,8 @@
                     new = new * fl[LO_AT]
                 if j > 1:
                     new = new * fl[HI_AT]
-                out, index_out = put(c, j)
-                out[(*index_out, rows, slice(None))] = new
+                for out, index_out in put(c, j):
+                    out[(*index_out, rows, slice(None))] = new
 
 
 def two_steps(first_step, perm_at):
@@ -104,7 +104,8 @@
         labels, rest = (rest[:1], rest[1:]) if first_step == 0 else ((), rest)
         mid, out, coef = rest[0], rest[1:-1], rest[-1]
         for ref in labels:
-            out[0][8] = ref[...].astype(F32)
+            out[0][16] = ref[1].astype(F32)
+            out[1][16] = ref[0].astype(F32)
         planes = [plow[(*perm_at, 0)], plow[(*perm_at, 1)], pmid[0], pmid[1]]
         planes += [phigh[(*perm_at, 0)], phigh[(*perm_at, 1)]]
         face_weights(planes, coef)
@@ -112,22 +113,23 @@
         def field(f, carry):
             def source(c, j):
                 k = f * 4 + c
+                if first_step == 0:
+                    if j < 0:
+                        return low, (k, j + 2)
+                    return (high, (k, j - 2)) if j > 1 else (own, (k, j))
                 if j < 0:
-                    return low, (k, j + 2)
-                if j > 1:
-                    return high, (k, j - 2)
-                return own, (k, j)
+                    return low, (2 * k + j + 2,)
+                return (high, (2 * k + j - 2,)) if j > 1 else (own, (2 * k + j,))
 
             def middle(c, j):
-                return mid, (f * 4 + c, j + 1)
+                return [(mid, (f * 4 + c, j + 1))]
 
             def last(c, j):
-                if len(out) == 1:
-                    return out[0], (f * 4 + c, j)
-                return out[j], (f * 4 + c,)
+                k = f * 4 + c
+                return [(x, (2 * k + j,)) for x in out] if first_step == 0 else [(out[j], (k,))]
 
             advance(f, first_step, source, middle, coef, -1, 4, fl, it)
-            advance(f, first_step + 1, middle, last, coef, 0, 2, fl, it)
+            advance(f, first_step + 1, lambda c, j: middle(c, j)[0], last, coef, 0, 2, fl, it)
             return carry
 
         lax.fori_loop(0, 2, field, 0)
@@ -156,10 +158,10 @@
         if stage == 4:
             return (s4a, (k,)) if j == 0 else (s4b, (k,))
         if j < 0:
-            return low2, (k, 1)
+            return low2, (2 * k + 1,)
         if j > 1:
-            return high2, (k, 0)
-        return s2, (k, j)
+            return high2, (2 * k,)
+        return s2, (2 * k + j,)
 
     for r in range(0, wide, ROWS):
         rows = pl.ds(r, ROWS)
@@ -218,7 +220,7 @@
         rows = pl.ds(pl.multiple_of(k * 8, 8), 8)
         cells = [(out[j, rows, :], perm[j, rows, :], labels[j, rows, :]) for j in range(2)]
         for j, far, names, at in ((0, low0, low2, 1), (1, high0, high2, 0)):
-            cells.append((half[j, rows, :], far[8, at, rows, :], names[8, at, rows, :].astype(jnp.int32)))
+            cells.append((half[j, rows, :], far[8, at, rows, :], names[16, rows, :].astype(jnp.int32)))
         left, right = [], []
         for g, weight, label in cells:
             value = g * weight * fl[NORM_AT]
@@ -252,7 +254,7 @@
             return (low4, s4a, s4b, high4)[j + 1], (f * 4 + c,)
 
         def target(c, j):
-            return out, (c, j)
+            return [(out, (c, j))]
 
         advance(f, STEPS - 1, source, target, coef, 0, 2, fl, it)
 
@@ -282,11 +284,13 @@
     return lax.ppermute(block_high, "space", forward), lax.ppermute(block_low, "space", backward)
 
 
+def gather(x, axis, groups):
+    copies = jnp.broadcast_to(x[None], (len(groups[0]), *x.shape))
+    return lax.all_to_all(copies, axis, 0, 0, axis_index_groups=groups, tiled=True)
+
+
 def sum_over(x, axis, groups):
-    n = len(groups[0])
-    copies = jnp.broadcast_to(x[None], (n, *x.shape))
-    got = lax.all_to_all(copies, axis, 0, 0, axis_index_groups=groups, tiled=True)
-    return jnp.sum(got, axis=0)
+    return jnp.sum(gather(x, axis, groups), axis=0)
 
 
 def on_device(
@@ -325,11 +329,11 @@
     low0, high0 = neighbours(s0, s0)
     plane = (8, wide, deep)
     coef = (4, 7, wide, deep)
-    t1, s2 = call(
+    t1, s2, s2_back = call(
         two_steps(0, (8,)), [s0, low0, high0, low0, permeability, high0, labels], [fl, it],
-        [(8, 4, wide, deep), (9, 2, wide, deep)], [coef], "steps_1_2", 20_000_000,
-    )
-    low2, high2 = neighbours(s2, s2)
+        [(8, 4, wide, deep), (17, wide, deep), (17, wide, deep)], [coef], "steps_1_2", 20_000_000,
+    )
+    low2, high2 = neighbours(s2_back, s2)
     t3, s4a, s4b = call(
         two_steps(2, (8,)), [s2, low2, high2, low0, permeability, high0], [fl, it],
         [(8, 4, wide, deep), plane, plane], [coef], "steps_3_4", 20_000_000,
@@ -348,7 +352,9 @@
         last_step, [low0, permeability, high0, low4, s4a, s4b, high4], [fl, it],
         [(4, 2, wide, deep)] * 2, [(2, 7, wide, deep)], "step_5", 10_000_000,
     )
-    bins = sum_over(bins, "exp", [list(range(exps))])
+    got = gather(bins, "exp", [list(range(exps))])
+    got, conc, sens = lax.optimization_barrier((got, conc, sens))
+    bins = jnp.sum(got, axis=0)
     return conc[None], sens[None], bins.reshape(-1)
 
 

time: 104 us -> 103 us (level)
  blocking collectives: 43.8 us -> 23.6 us
  starting transfers between devices: 18.1 us -> 31.1 us
  waiting for transfers between devices: 26 us -> 30.8 us
    all_to_all x3 -> x2, blocking collectives: 43.8 us -> 23.6 us  [gather(): lax.all_to_all(copies, axis, 0, 0, axis_index_groups=groups, tiled=True)]
    all_to_all x0 -> x1, starting transfers between devices: none -> 13 us  [gather(): lax.all_to_all(copies, axis, 0, 0, axis_index_groups=groups, tiled=True)]
    all_to_all x0 -> x1, waiting for transfers between devices: none -> 5.56 us  [gather(): lax.all_to_all(copies, axis, 0, 0, axis_index_groups=groups, tiled=True)]
  transfers between devices with their start and end apart: 6 -> 7, of which waited for: 4 -> 5; matrix products, arithmetic and copies ran while one was open for 1% -> 2% of each run, Pallas kernels for 0% -> 2%
where the time goes in v4:
time: 103 us; the launch traced here: 102 us
  starting transfers between devices  31.1 us (30%)
  waiting for transfers between devices  30.8 us (30%)
  blocking collectives  23.6 us (23%)
  Pallas kernels  10.1 us (10%)
  between operations  2.73 us (3%)
  other arithmetic  1.97 us (2%)
  local copies, waits for them, and re-layouts  1.94 us (2%)
    all_to_all x2, blocking collectives, gather(): lax.all_to_all(copies, axis, 0, 0, axis_index_groups=groups, tiled=True)  23.6 us
    ppermute x3, waiting for transfers between devices, neighbours(): lax.ppermute(block_low, 'space', backward)  16 us
    all_to_all x1, starting transfers between devices, gather(): lax.all_to_all(copies, axis, 0, 0, axis_index_groups=groups, tiled=True)  13 us
    ppermute x3, starting transfers between devices, neighbours(): lax.ppermute(block_low, 'space', backward)  10.6 us
    pallas_call x4, Pallas kernels, call(): pl.pallas_call(kernel, out_shape=[jax.ShapeDtypeStruct(s, F32) for s in o...  10.1 us
    ppermute x3, waiting for transfers between devices, neighbours(): lax.ppermute(block_high, 'space', forward)  9.32 us
    ppermute x3, starting transfers between devices, neighbours(): lax.ppermute(block_high, 'space', forward)  7.47 us
    all_to_all x1, waiting for transfers between devices, gather(): lax.all_to_all(copies, axis, 0, 0, axis_index_groups=groups, tiled=True)  5.56 us
  transfers between devices with their start and end apart: 7, of which 5 were waited for; matrix products, arithmetic and copies ran while one was open for 2% of the time, Pallas kernels for 2%

profile of v4, /device:TPU:65, one launch (start us, length us, event | category | flops | bytes accessed | tf_op | source)
XLA Modules:
  0.0 102.3 jit_solution(11964609882673760097)
XLA Ops:
  0.6 1.1 %pad_maximum_fusion.own.s0 = f32[9,2,64,128]{3,2,1,0:T(8,128)S(1)} fusion(f32[1,2,64,128]{3,2,1,0:T(8,128)} %bitcast.17, f32[4,2,64,128]{3,2,1,0:T(8,128)} %bitcast.18, f32[4,2,64,128]{3,2,1,0:T(8,128)} %bitcast.19), kind=kLoop, calls=%fused_computation | loop fusion | flops 294912 | bytes 1179648 | tf_op jit(solution)/shard_map/concatenate | solution.py:328
  1.7 3.5 %collective-permute-start.1 = (f32[9,2,64,128]{3,2,1,0:T(8,128)S(1)}, f32[9,2,64,128]{3,2,1,0:T(8,128)S(1)}, u32[]{:S(2)}, u32[]{:S(2)}) collective-permute-start(f32[9,2,64,128]{3,2,1,0:T(8,128)S(1)} %pad_maximum_fusion.own.s0), channel_id=1, source_target_pairs={{1,0},{2,1},{3,2},{4,3},{5,4},{6,5},{7,6},{8,7},{9,8},{10,9},{11,1... | collective-permute-start | bytes 1769480 | tf_op jit(solution)/shard_map/ppermute | solution.py:284
  5.2 1.9 %collective-permute-start = (f32[9,2,64,128]{3,2,1,0:T(8,128)S(1)}, f32[9,2,64,128]{3,2,1,0:T(8,128)S(1)}, u32[]{:S(2)}, u32[]{:S(2)}) collective-permute-start(f32[9,2,64,128]{3,2,1,0:T(8,128)S(1)} %pad_maximum_fusion.own.s0), channel_id=1, source_target_pairs={{0,1},{1,2},{2,3},{3,4},{4,5},{5,6},{6,7},{7,8},{8,9},{9,10},{10,1... | collective-permute-start | bytes 1769480 | tf_op jit(solution)/shard_map/ppermute | solution.py:284
  7.2 0.0 copy-start.2
  7.2 0.0 copy-start.3
  7.2 0.1 copy.23
  7.3 0.6 copy-done.2
  7.9 0.0 copy-done.3
  7.9 0.0 copy-start.4
  7.9 0.0 copy-start.1
  7.9 0.1 fusion.1
  8.0 0.0 copy-start
  8.0 0.1 copy.24
  10.1 0.1 copy.27
  10.2 0.1 reshape.20
  10.3 0.1 copy.25
  10.4 0.1 copy.26
  10.5 0.1 reshape.19
  10.6 0.0 copy-done.4
  10.6 0.1 concatenate.6.fl
  10.6 0.1 pad_add_fusion.it
  10.7 7.1 %collective-permute-done.1.high.phigh.high0 = f32[9,2,64,128]{3,2,1,0:T(8,128)S(1)} collective-permute-done((f32[9,2,64,128]{3,2,1,0:T(8,128)S(1)}, f32[9,2,64,128]{3,2,1,0:T(8,128)S(1)}, u32[]{:S(2)}, u32[]{:S(2)}) %collective-permute-start.1) | collective-permute-done | bytes 589856 | tf_op jit(solution)/shard_map/ppermute | solution.py:284
  17.8 5.3 %collective-permute-done.low.plow.low0 = f32[9,2,64,128]{3,2,1,0:T(8,128)S(1)} collective-permute-done((f32[9,2,64,128]{3,2,1,0:T(8,128)S(1)}, f32[9,2,64,128]{3,2,1,0:T(8,128)S(1)}, u32[]{:S(2)}, u32[]{:S(2)}) %collective-permute-start) | collective-permute-done | bytes 589856 | tf_op jit(solution)/shard_map/ppermute | solution.py:284
  23.1 0.0 copy-done.1
  23.1 0.0 copy-done
  23.1 2.2 %steps_1_2.1 = (f32[8,4,64,128]{3,2,1,0:T(8,128)S(1)}, f32[17,64,128]{2,1,0:T(8,128)S(1)}, f32[17,64,128]{2,1,0:T(8,128)S(1)}) custom-call(f32[44]{0:T(128)S(1)} %concatenate.6.fl, s32[3]{0:T(128)S(1)} %pad_add_fusion.it, f32[9,2,64,128]{3,2,1,0:T(8,128)S(1)} %pad_maximum_fusion.own.s0, f32[9,2,64,128]{3,2,1,0:T(8,128)S(1)} %collective-permute-done.low.plow.low0, ...), custom_call_target="tpu_custom_call" | custom-call | flops 20000000 | bytes 5242880 | tf_op jit(solution)/shard_map/steps_1_2/pallas_call | solution.py:268
  25.3 1.9 %collective-permute-start.3 = (f32[17,64,128]{2,1,0:T(8,128)S(1)}, f32[17,64,128]{2,1,0:T(8,128)S(1)}, u32[]{:S(2)}, u32[]{:S(2)}) collective-permute-start(f32[17,64,128]{2,1,0:T(8,128)S(1)} %get-tuple-element.19), channel_id=1, source_target_pairs={{1,0},{2,1},{3,2},{4,3},{5,4},{6,5},{7,6},{8,7},{9,8},{10,9},{11,1... | collective-permute-start | bytes 1671176 | tf_op jit(solution)/shard_map/ppermute | solution.py:284
  27.2 3.4 %collective-permute-start.2 = (f32[17,64,128]{2,1,0:T(8,128)S(1)}, f32[17,64,128]{2,1,0:T(8,128)S(1)}, u32[]{:S(2)}, u32[]{:S(2)}) collective-permute-start(f32[17,64,128]{2,1,0:T(8,128)S(1)} %get-tuple-element.18.own.s2), channel_id=1, source_target_pairs={{0,1},{1,2},{2,3},{3,4},{4,5},{5,6},{6,7},{7,8},{8,9},{9,10},{10,1... | collective-permute-start | bytes 1671176 | tf_op jit(solution)/shard_map/ppermute | solution.py:284
  30.6 8.8 %collective-permute-done.3.high.high2 = f32[17,64,128]{2,1,0:T(8,128)S(1)} collective-permute-done((f32[17,64,128]{2,1,0:T(8,128)S(1)}, f32[17,64,128]{2,1,0:T(8,128)S(1)}, u32[]{:S(2)}, u32[]{:S(2)}) %collective-permute-start.3) | collective-permute-done | bytes 557088 | tf_op jit(solution)/shard_map/ppermute | solution.py:284
  39.5 4.0 %collective-permute-done.2.low.low2 = f32[17,64,128]{2,1,0:T(8,128)S(1)} collective-permute-done((f32[17,64,128]{2,1,0:T(8,128)S(1)}, f32[17,64,128]{2,1,0:T(8,128)S(1)}, u32[]{:S(2)}, u32[]{:S(2)}) %collective-permute-start.2) | collective-permute-done | bytes 557088 | tf_op jit(solution)/shard_map/ppermute | solution.py:284
  43.5 2.3 %steps_3_4.1 = (f32[8,4,64,128]{3,2,1,0:T(8,128)S(1)}, f32[8,64,128]{2,1,0:T(8,128)S(1)}, f32[8,64,128]{2,1,0:T(8,128)S(1)}) custom-call(f32[44]{0:T(128)S(1)} %concatenate.6.fl, s32[3]{0:T(128)S(1)} %pad_add_fusion.it, f32[17,64,128]{2,1,0:T(8,128)S(1)} %get-tuple-element.18.own.s2, f32[17,64,128]{2,1,0:T(8,128)S(1)} %collective-permute-done.2.low.low2, ...), custom_call_target="tpu_custom_call" | custom-call | flops 20000000 | bytes 4489216 | tf_op jit(solution)/shard_map/steps_3_4/pallas_call | solution.py:268
  45.8 3.8 %gradient.1 = f32[4,128]{1,0:T(4,128)S(1)} custom-call(f32[44]{0:T(128)S(1)} %concatenate.6.fl, f32[9,2,64,128]{3,2,1,0:T(8,128)S(1)} %pad_maximum_fusion.own.s0, f32[9,2,64,128]{3,2,1,0:T(8,128)S(1)} %collective-permute-done.low.plow.low0, f32[9,2,64,128]{3,2,1,0:T(8,128)S(1)} %collective-permute-done.1.high.phigh.high0, ...), custom_call_target="tpu_custom_call" | custom-call | flops 20000000 | bytes 6195200 | tf_op jit(solution)/shard_map/gradient/pallas_call | solution.py:268
  49.6 6.5 %all_to_all.15 = f32[4,4,128]{2,1,0:T(4,128)S(1)} all-to-all(f32[4,4,128]{2,1,0:T(4,128)S(1)} %broadcast_in_dim.48), channel_id=1, replica_groups={{0,1,2,3},{4,5,6,7},{8,9,10,11},{12,13,14,15},{16,17,18,19},{20,21,22,2..., dimensions={0} | all-to-all | bytes 16384 | tf_op jit(solution)/shard_map/all_to_all | solution.py:289
  56.1 17.1 %all_to_all.16 = f32[8,4,128]{2,1,0:T(4,128)S(1)} all-to-all(f32[8,4,128]{2,1,0:T(4,128)S(1)} %broadcast_in_dim.49), channel_id=1, replica_groups={{0,4,8,12,16,20,24,28},{1,5,9,13,17,21,25,29},{2,6,10,14,18,22,26,30},{..., dimensions={0} | all-to-all | bytes 32768 | tf_op jit(solution)/shard_map/all_to_all | solution.py:289
  73.2 2.2 %collective-permute-start.4 = (f32[8,64,128]{2,1,0:T(8,128)S(1)}, f32[8,64,128]{2,1,0:T(8,128)S(1)}, u32[]{:S(2)}, u32[]{:S(2)}) collective-permute-start(f32[8,64,128]{2,1,0:T(8,128)S(1)} %get-tuple-element.24.s4b), channel_id=1, source_target_pairs={{0,1},{1,2},{2,3},{3,4},{4,5},{5,6},{6,7},{7,8},{8,9},{9,10},{10,1... | collective-permute-start | bytes 786440 | tf_op jit(solution)/shard_map/ppermute | solution.py:284
  75.4 5.2 %collective-permute-start.5 = (f32[8,64,128]{2,1,0:T(8,128)S(1)}, f32[8,64,128]{2,1,0:T(8,128)S(1)}, u32[]{:S(2)}, u32[]{:S(2)}) collective-permute-start(f32[8,64,128]{2,1,0:T(8,128)S(1)} %get-tuple-element.25.s4a), channel_id=1, source_target_pairs={{1,0},{2,1},{3,2},{4,3},{5,4},{6,5},{7,6},{8,7},{9,8},{10,9},{11,1... | collective-permute-start | bytes 786440 | tf_op jit(solution)/shard_map/ppermute | solution.py:284
  80.6 0.6 broadcast_in_dim.50
  81.2 13.0 %all-to-all-start.2 = ((f32[16,4,128]{2,1,0:T(4,128)}), f32[16,4,128]{2,1,0:T(4,128)S(1)}, u32[]{:S(2)}, u32[]{:S(2)}) async-start(f32[16,4,128]{2,1,0:T(4,128)} %broadcast_in_dim.50), calls=%async_computation.2 | async-start | bytes 65536 | tf_op jit(solution)/shard_map/all_to_all | solution.py:289
  94.3 0.0 collective-permute-done.4.low4
  94.3 0.0 collective-permute-done.5.high4
  94.3 1.8 %step_5.1 = (f32[4,2,64,128]{3,2,1,0:T(8,128)}, f32[4,2,64,128]{3,2,1,0:T(8,128)}) custom-call(f32[44]{0:T(128)S(1)} %concatenate.6.fl, s32[3]{0:T(128)S(1)} %pad_add_fusion.it, f32[9,2,64,128]{3,2,1,0:T(8,128)S(1)} %collective-permute-done.low.plow.low0, f32[2,64,128]{2,1,0:T(8,128)S(1)} %copy-done, ...), custom_call_target="tpu_custom_call" | custom-call | flops 10000000 | bytes 2818048 | tf_op jit(solution)/shard_map/step_5/pallas_call | solution.py:268
  96.1 5.6 %all-to-all-done.2 = f32[16,4,128]{2,1,0:T(4,128)S(1)} async-done(((f32[16,4,128]{2,1,0:T(4,128)}), f32[16,4,128]{2,1,0:T(4,128)S(1)}, u32[]{:S(2)}, u32[]{:S(2)}) %all-to-all-start.2) | async-done | bytes 32800 | tf_op jit(solution)/shard_map/all_to_all | solution.py:289
  101.7 0.6 reduce_sum.39
  (9 shorter events, 0.1 us)
Async XLA Ops:
  1.7 16.1 %collective-permute-start.1 = (f32[9,2,64,128]{3,2,1,0:T(8,128)S(1)}, f32[9,2,64,128]{3,2,1,0:T(8,128)S(1)}, u32[]{:S(2)}, u32[]{:S(2)}) collective-permute-start(f32[9,2,64,128]{3,2,1,0:T(8,128)S(1)} %pad_maximum_fusion.own.s0), channel_id=1, source_target_pairs={{1,0},{2,1},{3,2},{4,3},{5,4},{6,5},{7,6},{8,7},{9,8},{10,9},{11,1... | collective-permute-start | bytes 1769480 | tf_op jit(solution)/shard_map/ppermute | solution.py:284
  5.2 17.9 %collective-permute-start = (f32[9,2,64,128]{3,2,1,0:T(8,128)S(1)}, f32[9,2,64,128]{3,2,1,0:T(8,128)S(1)}, u32[]{:S(2)}, u32[]{:S(2)}) collective-permute-start(f32[9,2,64,128]{3,2,1,0:T(8,128)S(1)} %pad_maximum_fusion.own.s0), channel_id=1, source_target_pairs={{0,1},{1,2},{2,3},{3,4},{4,5},{5,6},{6,7},{7,8},{8,9},{9,10},{10,1... | collective-permute-start | bytes 1769480 | tf_op jit(solution)/shard_map/ppermute | solution.py:284
  7.2 0.7 copy-start.2
  7.2 0.7 copy-start.3
  7.9 2.7 %copy-start.4 = (f32[4]{0:T(128)S(1)}, f32[4]{0:T(128)}, u32[]{:S(2)}) copy-start(f32[4]{0:T(128)} %param.14) | copy-start | bytes 52
  7.9 15.2 %copy-start.1 = (s32[2,64,128]{2,1,0:T(8,128)S(1)}, s32[2,64,128]{2,1,0:T(8,128)}, u32[]{:S(2)}) copy-start(s32[2,64,128]{2,1,0:T(8,128)} %labels.1) | copy-start | bytes 196612
  8.0 15.1 %copy-start = (f32[2,64,128]{2,1,0:T(8,128)S(1)}, f32[2,64,128]{2,1,0:T(8,128)}, u32[]{:S(2)}) copy-start(f32[2,64,128]{2,1,0:T(8,128)} %perm.3) | copy-start | bytes 196612
  25.3 14.1 %collective-permute-start.3 = (f32[17,64,128]{2,1,0:T(8,128)S(1)}, f32[17,64,128]{2,1,0:T(8,128)S(1)}, u32[]{:S(2)}, u32[]{:S(2)}) collective-permute-start(f32[17,64,128]{2,1,0:T(8,128)S(1)} %get-tuple-element.19), channel_id=1, source_target_pairs={{1,0},{2,1},{3,2},{4,3},{5,4},{6,5},{7,6},{8,7},{9,8},{10,9},{11,1... | collective-permute-start | bytes 1671176 | tf_op jit(solution)/shard_map/ppermute | solution.py:284
  27.2 16.3 %collective-permute-start.2 = (f32[17,64,128]{2,1,0:T(8,128)S(1)}, f32[17,64,128]{2,1,0:T(8,128)S(1)}, u32[]{:S(2)}, u32[]{:S(2)}) collective-permute-start(f32[17,64,128]{2,1,0:T(8,128)S(1)} %get-tuple-element.18.own.s2), channel_id=1, source_target_pairs={{0,1},{1,2},{2,3},{3,4},{4,5},{5,6},{6,7},{7,8},{8,9},{9,10},{10,1... | collective-permute-start | bytes 1671176 | tf_op jit(solution)/shard_map/ppermute | solution.py:284
  73.2 21.1 %collective-permute-start.4 = (f32[8,64,128]{2,1,0:T(8,128)S(1)}, f32[8,64,128]{2,1,0:T(8,128)S(1)}, u32[]{:S(2)}, u32[]{:S(2)}) collective-permute-start(f32[8,64,128]{2,1,0:T(8,128)S(1)} %get-tuple-element.24.s4b), channel_id=1, source_target_pairs={{0,1},{1,2},{2,3},{3,4},{4,5},{5,6},{6,7},{7,8},{8,9},{9,10},{10,1... | collective-permute-start | bytes 786440 | tf_op jit(solution)/shard_map/ppermute | solution.py:284
  75.4 18.9 %collective-permute-start.5 = (f32[8,64,128]{2,1,0:T(8,128)S(1)}, f32[8,64,128]{2,1,0:T(8,128)S(1)}, u32[]{:S(2)}, u32[]{:S(2)}) collective-permute-start(f32[8,64,128]{2,1,0:T(8,128)S(1)} %get-tuple-element.25.s4a), channel_id=1, source_target_pairs={{1,0},{2,1},{3,2},{4,3},{5,4},{6,5},{7,6},{8,7},{9,8},{10,9},{11,1... | collective-permute-start | bytes 786440 | tf_op jit(solution)/shard_map/ppermute | solution.py:284
  81.2 20.4 %all-to-all-start.2 = ((f32[16,4,128]{2,1,0:T(4,128)}), f32[16,4,128]{2,1,0:T(4,128)S(1)}, u32[]{:S(2)}, u32[]{:S(2)}) async-start(f32[16,4,128]{2,1,0:T(4,128)} %broadcast_in_dim.50), calls=%async_computation.2 | async-start | bytes 65536 | tf_op jit(solution)/shard_map/all_to_all | solution.py:289

commit v5 on v4

--- a/solution.py
+++ b/solution.py
@@ -99,16 +99,16 @@
                     out[(*index_out, rows, slice(None))] = new
 
 
-def two_steps(first_step, perm_at):
-    def kernel(fl, it, own, low, high, plow, pmid, phigh, *rest):
-        labels, rest = (rest[:1], rest[1:]) if first_step == 0 else ((), rest)
-        mid, out, coef = rest[0], rest[1:-1], rest[-1]
-        for ref in labels:
-            out[0][16] = ref[1].astype(F32)
-            out[1][16] = ref[0].astype(F32)
-        planes = [plow[(*perm_at, 0)], plow[(*perm_at, 1)], pmid[0], pmid[1]]
-        planes += [phigh[(*perm_at, 0)], phigh[(*perm_at, 1)]]
-        face_weights(planes, coef)
+def two_steps(first_step):
+    def kernel(fl, it, own, low, high, *rest):
+        if first_step == 0:
+            labels, pmid, mid, *out, coef = rest
+            out[0][16] = labels[1].astype(F32)
+            out[1][16] = labels[0].astype(F32)
+            planes = [low[8, 0], low[8, 1], pmid[0], pmid[1], high[8, 0], high[8, 1]]
+            face_weights(planes, coef)
+        else:
+            coef, mid, *out = rest
 
         def field(f, carry):
             def source(c, j):
@@ -329,14 +329,14 @@
     low0, high0 = neighbours(s0, s0)
     plane = (8, wide, deep)
     coef = (4, 7, wide, deep)
-    t1, s2, s2_back = call(
-        two_steps(0, (8,)), [s0, low0, high0, low0, permeability, high0, labels], [fl, it],
-        [(8, 4, wide, deep), (17, wide, deep), (17, wide, deep)], [coef], "steps_1_2", 20_000_000,
+    t1, s2, s2_back, weights = call(
+        two_steps(0), [s0, low0, high0, labels, permeability], [fl, it],
+        [(8, 4, wide, deep), (17, wide, deep), (17, wide, deep), coef], [], "steps_1_2", 20_000_000,
     )
     low2, high2 = neighbours(s2_back, s2)
     t3, s4a, s4b = call(
-        two_steps(2, (8,)), [s2, low2, high2, low0, permeability, high0], [fl, it],
-        [(8, 4, wide, deep), plane, plane], [coef], "steps_3_4", 20_000_000,
+        two_steps(2), [s2, low2, high2, weights], [fl, it],
+        [(8, 4, wide, deep), plane, plane], [], "steps_3_4", 20_000_000,
     )
     bins, = call(
         gradient, [s0, low0, high0, t1, s2, low2, high2, t3, s4a, s4b, permeability, labels], [fl],

time: 103 us -> 103 us (level)
  no operation moved by 1% of the time
where the time goes in v5:
time: 103 us; the launch traced here: 102 us
  starting transfers between devices  31.1 us (30%)
  waiting for transfers between devices  30.8 us (30%)
  blocking collectives  23.6 us (23%)
  Pallas kernels  9.9 us (10%)
  between operations  2.73 us (3%)
  other arithmetic  1.97 us (2%)
  local copies, waits for them, and re-layouts  1.94 us (2%)
    all_to_all x2, blocking collectives, gather(): lax.all_to_all(copies, axis, 0, 0, axis_index_groups=groups, tiled=True)  23.6 us
    ppermute x3, waiting for transfers between devices, neighbours(): lax.ppermute(block_low, 'space', backward)  16 us
    all_to_all x1, starting transfers between devices, gather(): lax.all_to_all(copies, axis, 0, 0, axis_index_groups=groups, tiled=True)  13 us
    ppermute x3, starting transfers between devices, neighbours(): lax.ppermute(block_low, 'space', backward)  10.6 us
    pallas_call x4, Pallas kernels, call(): pl.pallas_call(kernel, out_shape=[jax.ShapeDtypeStruct(s, F32) for s in o...  9.9 us
    ppermute x3, waiting for transfers between devices, neighbours(): lax.ppermute(block_high, 'space', forward)  9.32 us
    ppermute x3, starting transfers between devices, neighbours(): lax.ppermute(block_high, 'space', forward)  7.47 us
    all_to_all x1, waiting for transfers between devices, gather(): lax.all_to_all(copies, axis, 0, 0, axis_index_groups=groups, tiled=True)  5.56 us
  transfers between devices with their start and end apart: 7, of which 5 were waited for; matrix products, arithmetic and copies ran while one was open for 2% of the time, Pallas kernels for 2%

profile of v5, /device:TPU:65, one launch (start us, length us, event | category | flops | bytes accessed | tf_op | source)
XLA Modules:
  0.0 102.1 jit_solution(2082663820634970889)
XLA Ops:
  0.6 1.1 %pad_maximum_fusion.own.s0 = f32[9,2,64,128]{3,2,1,0:T(8,128)S(1)} fusion(f32[1,2,64,128]{3,2,1,0:T(8,128)} %bitcast.17, f32[4,2,64,128]{3,2,1,0:T(8,128)} %bitcast.18, f32[4,2,64,128]{3,2,1,0:T(8,128)} %bitcast.19), kind=kLoop, calls=%fused_computation | loop fusion | flops 294912 | bytes 1179648 | tf_op jit(solution)/shard_map/concatenate | solution.py:328
  1.7 3.5 %collective-permute-start.1 = (f32[9,2,64,128]{3,2,1,0:T(8,128)S(1)}, f32[9,2,64,128]{3,2,1,0:T(8,128)S(1)}, u32[]{:S(2)}, u32[]{:S(2)}) collective-permute-start(f32[9,2,64,128]{3,2,1,0:T(8,128)S(1)} %pad_maximum_fusion.own.s0), channel_id=1, source_target_pairs={{1,0},{2,1},{3,2},{4,3},{5,4},{6,5},{7,6},{8,7},{9,8},{10,9},{11,1... | collective-permute-start | bytes 1769480 | tf_op jit(solution)/shard_map/ppermute | solution.py:284
  5.2 1.9 %collective-permute-start = (f32[9,2,64,128]{3,2,1,0:T(8,128)S(1)}, f32[9,2,64,128]{3,2,1,0:T(8,128)S(1)}, u32[]{:S(2)}, u32[]{:S(2)}) collective-permute-start(f32[9,2,64,128]{3,2,1,0:T(8,128)S(1)} %pad_maximum_fusion.own.s0), channel_id=1, source_target_pairs={{0,1},{1,2},{2,3},{3,4},{4,5},{5,6},{6,7},{7,8},{8,9},{9,10},{10,1... | collective-permute-start | bytes 1769480 | tf_op jit(solution)/shard_map/ppermute | solution.py:284
  7.2 0.0 copy-start.2
  7.2 0.0 copy-start.3
  7.2 0.1 copy.23
  7.3 0.6 copy-done.2
  7.9 0.0 copy-done.3
  7.9 0.0 copy-start.4
  7.9 0.0 copy-start.1
  7.9 0.1 fusion.1
  8.0 0.0 copy-start
  8.0 0.1 copy.24
  10.1 0.1 copy.27
  10.2 0.1 reshape.20
  10.3 0.1 copy.25
  10.4 0.1 copy.26
  10.5 0.1 reshape.19
  10.6 0.0 copy-done.4
  10.6 0.1 concatenate.6.fl
  10.6 0.1 pad_add_fusion.it
  10.7 7.1 %collective-permute-done.1.high.high0 = f32[9,2,64,128]{3,2,1,0:T(8,128)S(1)} collective-permute-done((f32[9,2,64,128]{3,2,1,0:T(8,128)S(1)}, f32[9,2,64,128]{3,2,1,0:T(8,128)S(1)}, u32[]{:S(2)}, u32[]{:S(2)}) %collective-permute-start.1) | collective-permute-done | bytes 589856 | tf_op jit(solution)/shard_map/ppermute | solution.py:284
  17.8 5.3 %collective-permute-done.low.low0 = f32[9,2,64,128]{3,2,1,0:T(8,128)S(1)} collective-permute-done((f32[9,2,64,128]{3,2,1,0:T(8,128)S(1)}, f32[9,2,64,128]{3,2,1,0:T(8,128)S(1)}, u32[]{:S(2)}, u32[]{:S(2)}) %collective-permute-start) | collective-permute-done | bytes 589856 | tf_op jit(solution)/shard_map/ppermute | solution.py:284
  23.1 0.0 copy-done.1
  23.1 0.0 copy-done
  23.1 2.2 %steps_1_2.1 = (f32[8,4,64,128]{3,2,1,0:T(8,128)S(1)}, f32[17,64,128]{2,1,0:T(8,128)S(1)}, f32[17,64,128]{2,1,0:T(8,128)S(1)}, f32[4,7,64,128]{3,2,1,0:T(8,128)S(1)}) custom-call(f32[44]{0:T(128)S(1)} %concatenate.6.fl, s32[3]{0:T(128)S(1)} %pad_add_fusion.it, f32[9,2,64,128]{3,2,1,0:T(8,128)S(1)} %pad_maximum_fusion.own.s0, ...), custom_call_target="tpu_custom_call" | custom-call | flops 20000000 | bytes 4980736 | tf_op jit(solution)/shard_map/steps_1_2/pallas_call | solution.py:268
  25.3 1.9 %collective-permute-start.3 = (f32[17,64,128]{2,1,0:T(8,128)S(1)}, f32[17,64,128]{2,1,0:T(8,128)S(1)}, u32[]{:S(2)}, u32[]{:S(2)}) collective-permute-start(f32[17,64,128]{2,1,0:T(8,128)S(1)} %get-tuple-element.20), channel_id=1, source_target_pairs={{1,0},{2,1},{3,2},{4,3},{5,4},{6,5},{7,6},{8,7},{9,8},{10,9},{11,1... | collective-permute-start | bytes 1671176 | tf_op jit(solution)/shard_map/ppermute | solution.py:284
  27.3 3.4 %collective-permute-start.2 = (f32[17,64,128]{2,1,0:T(8,128)S(1)}, f32[17,64,128]{2,1,0:T(8,128)S(1)}, u32[]{:S(2)}, u32[]{:S(2)}) collective-permute-start(f32[17,64,128]{2,1,0:T(8,128)S(1)} %get-tuple-element.19.own.s2), channel_id=1, source_target_pairs={{0,1},{1,2},{2,3},{3,4},{4,5},{5,6},{6,7},{7,8},{8,9},{9,10},{10,1... | collective-permute-start | bytes 1671176 | tf_op jit(solution)/shard_map/ppermute | solution.py:284
  30.6 8.8 %collective-permute-done.3.high.high2 = f32[17,64,128]{2,1,0:T(8,128)S(1)} collective-permute-done((f32[17,64,128]{2,1,0:T(8,128)S(1)}, f32[17,64,128]{2,1,0:T(8,128)S(1)}, u32[]{:S(2)}, u32[]{:S(2)}) %collective-permute-start.3) | collective-permute-done | bytes 557088 | tf_op jit(solution)/shard_map/ppermute | solution.py:284
  39.5 4.0 %collective-permute-done.2.low.low2 = f32[17,64,128]{2,1,0:T(8,128)S(1)} collective-permute-done((f32[17,64,128]{2,1,0:T(8,128)S(1)}, f32[17,64,128]{2,1,0:T(8,128)S(1)}, u32[]{:S(2)}, u32[]{:S(2)}) %collective-permute-start.2) | collective-permute-done | bytes 557088 | tf_op jit(solution)/shard_map/ppermute | solution.py:284
  43.5 2.1 %steps_3_4.1 = (f32[8,4,64,128]{3,2,1,0:T(8,128)S(1)}, f32[8,64,128]{2,1,0:T(8,128)S(1)}, f32[8,64,128]{2,1,0:T(8,128)S(1)}) custom-call(f32[44]{0:T(128)S(1)} %concatenate.6.fl, s32[3]{0:T(128)S(1)} %pad_add_fusion.it, f32[17,64,128]{2,1,0:T(8,128)S(1)} %get-tuple-element.19.own.s2, f32[17,64,128]{2,1,0:T(8,128)S(1)} %collective-permute-done.2.low.low2, ...), custom_call_target="tpu_custom_call" | custom-call | flops 20000000 | bytes 4161536 | tf_op jit(solution)/shard_map/steps_3_4/pallas_call | solution.py:268
  45.6 3.8 %gradient.1 = f32[4,128]{1,0:T(4,128)S(1)} custom-call(f32[44]{0:T(128)S(1)} %concatenate.6.fl, f32[9,2,64,128]{3,2,1,0:T(8,128)S(1)} %pad_maximum_fusion.own.s0, f32[9,2,64,128]{3,2,1,0:T(8,128)S(1)} %collective-permute-done.low.low0, f32[9,2,64,128]{3,2,1,0:T(8,128)S(1)} %collective-permute-done.1.high.high0, f32[8,4,64,128]{3,2,1,0:T(8,128)S(1)} %get-tuple-element.18.t1, ...), custom_call_target="tpu_custom_call" | custom-call | flops 20000000 | bytes 6195200 | tf_op jit(solution)/shard_map/gradient/pallas_call | solution.py:268
  49.4 6.5 %all_to_all.15 = f32[4,4,128]{2,1,0:T(4,128)S(1)} all-to-all(f32[4,4,128]{2,1,0:T(4,128)S(1)} %broadcast_in_dim.48), channel_id=1, replica_groups={{0,1,2,3},{4,5,6,7},{8,9,10,11},{12,13,14,15},{16,17,18,19},{20,21,22,2..., dimensions={0} | all-to-all | bytes 16384 | tf_op jit(solution)/shard_map/all_to_all | solution.py:289
  55.9 17.1 %all_to_all.16 = f32[8,4,128]{2,1,0:T(4,128)S(1)} all-to-all(f32[8,4,128]{2,1,0:T(4,128)S(1)} %broadcast_in_dim.49), channel_id=1, replica_groups={{0,4,8,12,16,20,24,28},{1,5,9,13,17,21,25,29},{2,6,10,14,18,22,26,30},{..., dimensions={0} | all-to-all | bytes 32768 | tf_op jit(solution)/shard_map/all_to_all | solution.py:289
  73.0 2.2 %collective-permute-start.4 = (f32[8,64,128]{2,1,0:T(8,128)S(1)}, f32[8,64,128]{2,1,0:T(8,128)S(1)}, u32[]{:S(2)}, u32[]{:S(2)}) collective-permute-start(f32[8,64,128]{2,1,0:T(8,128)S(1)} %get-tuple-element.26.s4b), channel_id=1, source_target_pairs={{0,1},{1,2},{2,3},{3,4},{4,5},{5,6},{6,7},{7,8},{8,9},{9,10},{10,1... | collective-permute-start | bytes 786440 | tf_op jit(solution)/shard_map/ppermute | solution.py:284
  75.2 5.2 %collective-permute-start.5 = (f32[8,64,128]{2,1,0:T(8,128)S(1)}, f32[8,64,128]{2,1,0:T(8,128)S(1)}, u32[]{:S(2)}, u32[]{:S(2)}) collective-permute-start(f32[8,64,128]{2,1,0:T(8,128)S(1)} %get-tuple-element.27.s4a), channel_id=1, source_target_pairs={{1,0},{2,1},{3,2},{4,3},{5,4},{6,5},{7,6},{8,7},{9,8},{10,9},{11,1... | collective-permute-start | bytes 786440 | tf_op jit(solution)/shard_map/ppermute | solution.py:284
  80.4 0.6 broadcast_in_dim.50
  81.0 13.0 %all-to-all-start.2 = ((f32[16,4,128]{2,1,0:T(4,128)}), f32[16,4,128]{2,1,0:T(4,128)S(1)}, u32[]{:S(2)}, u32[]{:S(2)}) async-start(f32[16,4,128]{2,1,0:T(4,128)} %broadcast_in_dim.50), calls=%async_computation.2 | async-start | bytes 65536 | tf_op jit(solution)/shard_map/all_to_all | solution.py:289
  94.1 0.0 collective-permute-done.4.low4
  94.1 0.0 collective-permute-done.5.high4
  94.1 1.8 %step_5.1 = (f32[4,2,64,128]{3,2,1,0:T(8,128)}, f32[4,2,64,128]{3,2,1,0:T(8,128)}) custom-call(f32[44]{0:T(128)S(1)} %concatenate.6.fl, s32[3]{0:T(128)S(1)} %pad_add_fusion.it, f32[9,2,64,128]{3,2,1,0:T(8,128)S(1)} %collective-permute-done.low.low0, f32[2,64,128]{2,1,0:T(8,128)S(1)} %copy-done, f32[9,2,64,128]{3,2,1,0:T(8,128)S(1)} %collective-permute-done.1.high.high0, ...), custom_call_target="tpu_custom_call" | custom-call | flops 10000000 | bytes 2818048 | tf_op jit(solution)/shard_map/step_5/pallas_call | solution.py:268
  95.9 5.6 %all-to-all-done.2 = f32[16,4,128]{2,1,0:T(4,128)S(1)} async-done(((f32[16,4,128]{2,1,0:T(4,128)}), f32[16,4,128]{2,1,0:T(4,128)S(1)}, u32[]{:S(2)}, u32[]{:S(2)}) %all-to-all-start.2) | async-done | bytes 32800 | tf_op jit(solution)/shard_map/all_to_all | solution.py:289
  101.5 0.6 reduce_sum.39
  (9 shorter events, 0.1 us)
Async XLA Ops:
  1.7 16.1 %collective-permute-start.1 = (f32[9,2,64,128]{3,2,1,0:T(8,128)S(1)}, f32[9,2,64,128]{3,2,1,0:T(8,128)S(1)}, u32[]{:S(2)}, u32[]{:S(2)}) collective-permute-start(f32[9,2,64,128]{3,2,1,0:T(8,128)S(1)} %pad_maximum_fusion.own.s0), channel_id=1, source_target_pairs={{1,0},{2,1},{3,2},{4,3},{5,4},{6,5},{7,6},{8,7},{9,8},{10,9},{11,1... | collective-permute-start | bytes 1769480 | tf_op jit(solution)/shard_map/ppermute | solution.py:284
  5.2 17.9 %collective-permute-start = (f32[9,2,64,128]{3,2,1,0:T(8,128)S(1)}, f32[9,2,64,128]{3,2,1,0:T(8,128)S(1)}, u32[]{:S(2)}, u32[]{:S(2)}) collective-permute-start(f32[9,2,64,128]{3,2,1,0:T(8,128)S(1)} %pad_maximum_fusion.own.s0), channel_id=1, source_target_pairs={{0,1},{1,2},{2,3},{3,4},{4,5},{5,6},{6,7},{7,8},{8,9},{9,10},{10,1... | collective-permute-start | bytes 1769480 | tf_op jit(solution)/shard_map/ppermute | solution.py:284
  7.2 0.7 copy-start.2
  7.2 0.7 copy-start.3
  7.9 2.7 %copy-start.4 = (f32[4]{0:T(128)S(1)}, f32[4]{0:T(128)}, u32[]{:S(2)}) copy-start(f32[4]{0:T(128)} %param.14) | copy-start | bytes 52
  7.9 15.2 %copy-start.1 = (s32[2,64,128]{2,1,0:T(8,128)S(1)}, s32[2,64,128]{2,1,0:T(8,128)}, u32[]{:S(2)}) copy-start(s32[2,64,128]{2,1,0:T(8,128)} %labels.1) | copy-start | bytes 196612
  8.0 15.1 %copy-start = (f32[2,64,128]{2,1,0:T(8,128)S(1)}, f32[2,64,128]{2,1,0:T(8,128)}, u32[]{:S(2)}) copy-start(f32[2,64,128]{2,1,0:T(8,128)} %perm.3) | copy-start | bytes 196612
  25.3 14.1 %collective-permute-start.3 = (f32[17,64,128]{2,1,0:T(8,128)S(1)}, f32[17,64,128]{2,1,0:T(8,128)S(1)}, u32[]{:S(2)}, u32[]{:S(2)}) collective-permute-start(f32[17,64,128]{2,1,0:T(8,128)S(1)} %get-tuple-element.20), channel_id=1, source_target_pairs={{1,0},{2,1},{3,2},{4,3},{5,4},{6,5},{7,6},{8,7},{9,8},{10,9},{11,1... | collective-permute-start | bytes 1671176 | tf_op jit(solution)/shard_map/ppermute | solution.py:284
  27.3 16.3 %collective-permute-start.2 = (f32[17,64,128]{2,1,0:T(8,128)S(1)}, f32[17,64,128]{2,1,0:T(8,128)S(1)}, u32[]{:S(2)}, u32[]{:S(2)}) collective-permute-start(f32[17,64,128]{2,1,0:T(8,128)S(1)} %get-tuple-element.19.own.s2), channel_id=1, source_target_pairs={{0,1},{1,2},{2,3},{3,4},{4,5},{5,6},{6,7},{7,8},{8,9},{9,10},{10,1... | collective-permute-start | bytes 1671176 | tf_op jit(solution)/shard_map/ppermute | solution.py:284
  73.0 21.1 %collective-permute-start.4 = (f32[8,64,128]{2,1,0:T(8,128)S(1)}, f32[8,64,128]{2,1,0:T(8,128)S(1)}, u32[]{:S(2)}, u32[]{:S(2)}) collective-permute-start(f32[8,64,128]{2,1,0:T(8,128)S(1)} %get-tuple-element.26.s4b), channel_id=1, source_target_pairs={{0,1},{1,2},{2,3},{3,4},{4,5},{5,6},{6,7},{7,8},{8,9},{9,10},{10,1... | collective-permute-start | bytes 786440 | tf_op jit(solution)/shard_map/ppermute | solution.py:284
  75.2 18.9 %collective-permute-start.5 = (f32[8,64,128]{2,1,0:T(8,128)S(1)}, f32[8,64,128]{2,1,0:T(8,128)S(1)}, u32[]{:S(2)}, u32[]{:S(2)}) collective-permute-start(f32[8,64,128]{2,1,0:T(8,128)S(1)} %get-tuple-element.27.s4a), channel_id=1, source_target_pairs={{1,0},{2,1},{3,2},{4,3},{5,4},{6,5},{7,6},{8,7},{9,8},{10,9},{11,1... | collective-permute-start | bytes 786440 | tf_op jit(solution)/shard_map/ppermute | solution.py:284
  81.0 20.4 %all-to-all-start.2 = ((f32[16,4,128]{2,1,0:T(4,128)}), f32[16,4,128]{2,1,0:T(4,128)S(1)}, u32[]{:S(2)}, u32[]{:S(2)}) async-start(f32[16,4,128]{2,1,0:T(4,128)} %broadcast_in_dim.50), calls=%async_computation.2 | async-start | bytes 65536 | tf_op jit(solution)/shard_map/all_to_all | solution.py:289

commit v6 on v5

--- a/solution.py
+++ b/solution.py
@@ -10,7 +10,7 @@
 STEPS = 5
 LABELS = 512
 TAU = 0.1
-ROWS = 16
+ROWS = 8
 F32 = jnp.float32
 
 A_AT, TS_AT, S_AT, LO_AT, HI_AT, DOSE_AT, NORM_AT = 0, 32, 36, 40, 41, 42, 43

time: 103 us -> 103 us (level)
  no operation moved by 1% of the time
where the time goes in v6:
time: 103 us; the launch traced here: 102 us
  starting transfers between devices  31.1 us (30%)
  waiting for transfers between devices  30.8 us (30%)
  blocking collectives  23.6 us (23%)
  Pallas kernels  10.2 us (10%)
  between operations  2.73 us (3%)
  other arithmetic  1.97 us (2%)
  local copies, waits for them, and re-layouts  1.94 us (2%)
    all_to_all x2, blocking collectives, gather(): lax.all_to_all(copies, axis, 0, 0, axis_index_groups=groups, tiled=True)  23.6 us
    ppermute x3, waiting for transfers between devices, neighbours(): lax.ppermute(block_low, 'space', backward)  16 us
    all_to_all x1, starting transfers between devices, gather(): lax.all_to_all(copies, axis, 0, 0, axis_index_groups=groups, tiled=True)  13 us
    ppermute x3, starting transfers between devices, neighbours(): lax.ppermute(block_low, 'space', backward)  10.6 us
    pallas_call x4, Pallas kernels, call(): pl.pallas_call(kernel, out_shape=[jax.ShapeDtypeStruct(s, F32) for s in o...  10.2 us
    ppermute x3, waiting for transfers between devices, neighbours(): lax.ppermute(block_high, 'space', forward)  9.32 us
    ppermute x3, starting transfers between devices, neighbours(): lax.ppermute(block_high, 'space', forward)  7.47 us
    all_to_all x1, waiting for transfers between devices, gather(): lax.all_to_all(copies, axis, 0, 0, axis_index_groups=groups, tiled=True)  5.55 us
  transfers between devices with their start and end apart: 7, of which 5 were waited for; matrix products, arithmetic and copies ran while one was open for 2% of the time, Pallas kernels for 2%

profile of v6, /device:TPU:65, one launch (start us, length us, event | category | flops | bytes accessed | tf_op | source)
XLA Modules:
  0.0 102.3 jit_solution(7499048977006240880)
XLA Ops:
  0.6 1.1 %pad_maximum_fusion.own.s0 = f32[9,2,64,128]{3,2,1,0:T(8,128)S(1)} fusion(f32[1,2,64,128]{3,2,1,0:T(8,128)} %bitcast.17, f32[4,2,64,128]{3,2,1,0:T(8,128)} %bitcast.18, f32[4,2,64,128]{3,2,1,0:T(8,128)} %bitcast.19), kind=kLoop, calls=%fused_computation | loop fusion | flops 294912 | bytes 1179648 | tf_op jit(solution)/shard_map/concatenate | solution.py:328
  1.7 3.5 %collective-permute-start.1 = (f32[9,2,64,128]{3,2,1,0:T(8,128)S(1)}, f32[9,2,64,128]{3,2,1,0:T(8,128)S(1)}, u32[]{:S(2)}, u32[]{:S(2)}) collective-permute-start(f32[9,2,64,128]{3,2,1,0:T(8,128)S(1)} %pad_maximum_fusion.own.s0), channel_id=1, source_target_pairs={{1,0},{2,1},{3,2},{4,3},{5,4},{6,5},{7,6},{8,7},{9,8},{10,9},{11,1... | collective-permute-start | bytes 1769480 | tf_op jit(solution)/shard_map/ppermute | solution.py:284
  5.2 1.9 %collective-permute-start = (f32[9,2,64,128]{3,2,1,0:T(8,128)S(1)}, f32[9,2,64,128]{3,2,1,0:T(8,128)S(1)}, u32[]{:S(2)}, u32[]{:S(2)}) collective-permute-start(f32[9,2,64,128]{3,2,1,0:T(8,128)S(1)} %pad_maximum_fusion.own.s0), channel_id=1, source_target_pairs={{0,1},{1,2},{2,3},{3,4},{4,5},{5,6},{6,7},{7,8},{8,9},{9,10},{10,1... | collective-permute-start | bytes 1769480 | tf_op jit(solution)/shard_map/ppermute | solution.py:284
  7.2 0.0 copy-start.2
  7.2 0.0 copy-start.3
  7.2 0.1 copy.23
  7.3 0.6 copy-done.2
  7.9 0.0 copy-done.3
  7.9 0.0 copy-start.4
  7.9 0.0 copy-start.1
  7.9 0.1 fusion.1
  8.0 0.0 copy-start
  8.0 0.1 copy.24
  10.1 0.1 copy.27
  10.2 0.1 reshape.20
  10.3 0.1 copy.25
  10.4 0.1 copy.26
  10.5 0.1 reshape.19
  10.6 0.0 copy-done.4
  10.6 0.1 concatenate.6.fl
  10.6 0.1 pad_add_fusion.it
  10.7 7.1 %collective-permute-done.1.high.high0 = f32[9,2,64,128]{3,2,1,0:T(8,128)S(1)} collective-permute-done((f32[9,2,64,128]{3,2,1,0:T(8,128)S(1)}, f32[9,2,64,128]{3,2,1,0:T(8,128)S(1)}, u32[]{:S(2)}, u32[]{:S(2)}) %collective-permute-start.1) | collective-permute-done | bytes 589856 | tf_op jit(solution)/shard_map/ppermute | solution.py:284
  17.8 5.3 %collective-permute-done.low.low0 = f32[9,2,64,128]{3,2,1,0:T(8,128)S(1)} collective-permute-done((f32[9,2,64,128]{3,2,1,0:T(8,128)S(1)}, f32[9,2,64,128]{3,2,1,0:T(8,128)S(1)}, u32[]{:S(2)}, u32[]{:S(2)}) %collective-permute-start) | collective-permute-done | bytes 589856 | tf_op jit(solution)/shard_map/ppermute | solution.py:284
  23.1 0.0 copy-done.1
  23.1 0.0 copy-done
  23.1 2.3 %steps_1_2.1 = (f32[8,4,64,128]{3,2,1,0:T(8,128)S(1)}, f32[17,64,128]{2,1,0:T(8,128)S(1)}, f32[17,64,128]{2,1,0:T(8,128)S(1)}, f32[4,7,64,128]{3,2,1,0:T(8,128)S(1)}) custom-call(f32[44]{0:T(128)S(1)} %concatenate.6.fl, s32[3]{0:T(128)S(1)} %pad_add_fusion.it, f32[9,2,64,128]{3,2,1,0:T(8,128)S(1)} %pad_maximum_fusion.own.s0, ...), custom_call_target="tpu_custom_call" | custom-call | flops 20000000 | bytes 4980736 | tf_op jit(solution)/shard_map/steps_1_2/pallas_call | solution.py:268
  25.4 1.9 %collective-permute-start.3 = (f32[17,64,128]{2,1,0:T(8,128)S(1)}, f32[17,64,128]{2,1,0:T(8,128)S(1)}, u32[]{:S(2)}, u32[]{:S(2)}) collective-permute-start(f32[17,64,128]{2,1,0:T(8,128)S(1)} %get-tuple-element.20), channel_id=1, source_target_pairs={{1,0},{2,1},{3,2},{4,3},{5,4},{6,5},{7,6},{8,7},{9,8},{10,9},{11,1... | collective-permute-start | bytes 1671176 | tf_op jit(solution)/shard_map/ppermute | solution.py:284
  27.3 3.4 %collective-permute-start.2 = (f32[17,64,128]{2,1,0:T(8,128)S(1)}, f32[17,64,128]{2,1,0:T(8,128)S(1)}, u32[]{:S(2)}, u32[]{:S(2)}) collective-permute-start(f32[17,64,128]{2,1,0:T(8,128)S(1)} %get-tuple-element.19.own.s2), channel_id=1, source_target_pairs={{0,1},{1,2},{2,3},{3,4},{4,5},{5,6},{6,7},{7,8},{8,9},{9,10},{10,1... | collective-permute-start | bytes 1671176 | tf_op jit(solution)/shard_map/ppermute | solution.py:284
  30.7 8.8 %collective-permute-done.3.high.high2 = f32[17,64,128]{2,1,0:T(8,128)S(1)} collective-permute-done((f32[17,64,128]{2,1,0:T(8,128)S(1)}, f32[17,64,128]{2,1,0:T(8,128)S(1)}, u32[]{:S(2)}, u32[]{:S(2)}) %collective-permute-start.3) | collective-permute-done | bytes 557088 | tf_op jit(solution)/shard_map/ppermute | solution.py:284
  39.5 4.0 %collective-permute-done.2.low.low2 = f32[17,64,128]{2,1,0:T(8,128)S(1)} collective-permute-done((f32[17,64,128]{2,1,0:T(8,128)S(1)}, f32[17,64,128]{2,1,0:T(8,128)S(1)}, u32[]{:S(2)}, u32[]{:S(2)}) %collective-permute-start.2) | collective-permute-done | bytes 557088 | tf_op jit(solution)/shard_map/ppermute | solution.py:284
  43.6 2.1 %steps_3_4.1 = (f32[8,4,64,128]{3,2,1,0:T(8,128)S(1)}, f32[8,64,128]{2,1,0:T(8,128)S(1)}, f32[8,64,128]{2,1,0:T(8,128)S(1)}) custom-call(f32[44]{0:T(128)S(1)} %concatenate.6.fl, s32[3]{0:T(128)S(1)} %pad_add_fusion.it, f32[17,64,128]{2,1,0:T(8,128)S(1)} %get-tuple-element.19.own.s2, f32[17,64,128]{2,1,0:T(8,128)S(1)} %collective-permute-done.2.low.low2, ...), custom_call_target="tpu_custom_call" | custom-call | flops 20000000 | bytes 4161536 | tf_op jit(solution)/shard_map/steps_3_4/pallas_call | solution.py:268
  45.7 4.0 %gradient.1 = f32[4,128]{1,0:T(4,128)S(1)} custom-call(f32[44]{0:T(128)S(1)} %concatenate.6.fl, f32[9,2,64,128]{3,2,1,0:T(8,128)S(1)} %pad_maximum_fusion.own.s0, f32[9,2,64,128]{3,2,1,0:T(8,128)S(1)} %collective-permute-done.low.low0, f32[9,2,64,128]{3,2,1,0:T(8,128)S(1)} %collective-permute-done.1.high.high0, f32[8,4,64,128]{3,2,1,0:T(8,128)S(1)} %get-tuple-element.18.t1, ...), custom_call_target="tpu_custom_call" | custom-call | flops 20000000 | bytes 6195200 | tf_op jit(solution)/shard_map/gradient/pallas_call | solution.py:268
  49.7 6.5 %all_to_all.15 = f32[4,4,128]{2,1,0:T(4,128)S(1)} all-to-all(f32[4,4,128]{2,1,0:T(4,128)S(1)} %broadcast_in_dim.48), channel_id=1, replica_groups={{0,1,2,3},{4,5,6,7},{8,9,10,11},{12,13,14,15},{16,17,18,19},{20,21,22,2..., dimensions={0} | all-to-all | bytes 16384 | tf_op jit(solution)/shard_map/all_to_all | solution.py:289
  56.2 17.1 %all_to_all.16 = f32[8,4,128]{2,1,0:T(4,128)S(1)} all-to-all(f32[8,4,128]{2,1,0:T(4,128)S(1)} %broadcast_in_dim.49), channel_id=1, replica_groups={{0,4,8,12,16,20,24,28},{1,5,9,13,17,21,25,29},{2,6,10,14,18,22,26,30},{..., dimensions={0} | all-to-all | bytes 32768 | tf_op jit(solution)/shard_map/all_to_all | solution.py:289
  73.3 2.2 %collective-permute-start.4 = (f32[8,64,128]{2,1,0:T(8,128)S(1)}, f32[8,64,128]{2,1,0:T(8,128)S(1)}, u32[]{:S(2)}, u32[]{:S(2)}) collective-permute-start(f32[8,64,128]{2,1,0:T(8,128)S(1)} %get-tuple-element.26.s4b), channel_id=1, source_target_pairs={{0,1},{1,2},{2,3},{3,4},{4,5},{5,6},{6,7},{7,8},{8,9},{9,10},{10,1... | collective-permute-start | bytes 786440 | tf_op jit(solution)/shard_map/ppermute | solution.py:284
  75.5 5.2 %collective-permute-start.5 = (f32[8,64,128]{2,1,0:T(8,128)S(1)}, f32[8,64,128]{2,1,0:T(8,128)S(1)}, u32[]{:S(2)}, u32[]{:S(2)}) collective-permute-start(f32[8,64,128]{2,1,0:T(8,128)S(1)} %get-tuple-element.27.s4a), channel_id=1, source_target_pairs={{1,0},{2,1},{3,2},{4,3},{5,4},{6,5},{7,6},{8,7},{9,8},{10,9},{11,1... | collective-permute-start | bytes 786440 | tf_op jit(solution)/shard_map/ppermute | solution.py:284
  80.7 0.6 broadcast_in_dim.50
  81.3 13.0 %all-to-all-start.2 = ((f32[16,4,128]{2,1,0:T(4,128)}), f32[16,4,128]{2,1,0:T(4,128)S(1)}, u32[]{:S(2)}, u32[]{:S(2)}) async-start(f32[16,4,128]{2,1,0:T(4,128)} %broadcast_in_dim.50), calls=%async_computation.2 | async-start | bytes 65536 | tf_op jit(solution)/shard_map/all_to_all | solution.py:289
  94.3 0.0 collective-permute-done.4.low4
  94.3 0.0 collective-permute-done.5.high4
  94.3 1.8 %step_5.1 = (f32[4,2,64,128]{3,2,1,0:T(8,128)}, f32[4,2,64,128]{3,2,1,0:T(8,128)}) custom-call(f32[44]{0:T(128)S(1)} %concatenate.6.fl, s32[3]{0:T(128)S(1)} %pad_add_fusion.it, f32[9,2,64,128]{3,2,1,0:T(8,128)S(1)} %collective-permute-done.low.low0, f32[2,64,128]{2,1,0:T(8,128)S(1)} %copy-done, f32[9,2,64,128]{3,2,1,0:T(8,128)S(1)} %collective-permute-done.1.high.high0, ...), custom_call_target="tpu_custom_call" | custom-call | flops 10000000 | bytes 2818048 | tf_op jit(solution)/shard_map/step_5/pallas_call | solution.py:268
  96.2 5.6 %all-to-all-done.2 = f32[16,4,128]{2,1,0:T(4,128)S(1)} async-done(((f32[16,4,128]{2,1,0:T(4,128)}), f32[16,4,128]{2,1,0:T(4,128)S(1)}, u32[]{:S(2)}, u32[]{:S(2)}) %all-to-all-start.2) | async-done | bytes 32800 | tf_op jit(solution)/shard_map/all_to_all | solution.py:289
  101.7 0.6 reduce_sum.39
  (9 shorter events, 0.1 us)
Async XLA Ops:
  1.7 16.1 %collective-permute-start.1 = (f32[9,2,64,128]{3,2,1,0:T(8,128)S(1)}, f32[9,2,64,128]{3,2,1,0:T(8,128)S(1)}, u32[]{:S(2)}, u32[]{:S(2)}) collective-permute-start(f32[9,2,64,128]{3,2,1,0:T(8,128)S(1)} %pad_maximum_fusion.own.s0), channel_id=1, source_target_pairs={{1,0},{2,1},{3,2},{4,3},{5,4},{6,5},{7,6},{8,7},{9,8},{10,9},{11,1... | collective-permute-start | bytes 1769480 | tf_op jit(solution)/shard_map/ppermute | solution.py:284
  5.2 17.9 %collective-permute-start = (f32[9,2,64,128]{3,2,1,0:T(8,128)S(1)}, f32[9,2,64,128]{3,2,1,0:T(8,128)S(1)}, u32[]{:S(2)}, u32[]{:S(2)}) collective-permute-start(f32[9,2,64,128]{3,2,1,0:T(8,128)S(1)} %pad_maximum_fusion.own.s0), channel_id=1, source_target_pairs={{0,1},{1,2},{2,3},{3,4},{4,5},{5,6},{6,7},{7,8},{8,9},{9,10},{10,1... | collective-permute-start | bytes 1769480 | tf_op jit(solution)/shard_map/ppermute | solution.py:284
  7.2 0.7 copy-start.2
  7.2 0.7 copy-start.3
  7.9 2.7 %copy-start.4 = (f32[4]{0:T(128)S(1)}, f32[4]{0:T(128)}, u32[]{:S(2)}) copy-start(f32[4]{0:T(128)} %param.14) | copy-start | bytes 52
  7.9 15.2 %copy-start.1 = (s32[2,64,128]{2,1,0:T(8,128)S(1)}, s32[2,64,128]{2,1,0:T(8,128)}, u32[]{:S(2)}) copy-start(s32[2,64,128]{2,1,0:T(8,128)} %labels.1) | copy-start | bytes 196612
  8.0 15.1 %copy-start = (f32[2,64,128]{2,1,0:T(8,128)S(1)}, f32[2,64,128]{2,1,0:T(8,128)}, u32[]{:S(2)}) copy-start(f32[2,64,128]{2,1,0:T(8,128)} %perm.3) | copy-start | bytes 196612
  25.4 14.1 %collective-permute-start.3 = (f32[17,64,128]{2,1,0:T(8,128)S(1)}, f32[17,64,128]{2,1,0:T(8,128)S(1)}, u32[]{:S(2)}, u32[]{:S(2)}) collective-permute-start(f32[17,64,128]{2,1,0:T(8,128)S(1)} %get-tuple-element.20), channel_id=1, source_target_pairs={{1,0},{2,1},{3,2},{4,3},{5,4},{6,5},{7,6},{8,7},{9,8},{10,9},{11,1... | collective-permute-start | bytes 1671176 | tf_op jit(solution)/shard_map/ppermute | solution.py:284
  27.3 16.3 %collective-permute-start.2 = (f32[17,64,128]{2,1,0:T(8,128)S(1)}, f32[17,64,128]{2,1,0:T(8,128)S(1)}, u32[]{:S(2)}, u32[]{:S(2)}) collective-permute-start(f32[17,64,128]{2,1,0:T(8,128)S(1)} %get-tuple-element.19.own.s2), channel_id=1, source_target_pairs={{0,1},{1,2},{2,3},{3,4},{4,5},{5,6},{6,7},{7,8},{8,9},{9,10},{10,1... | collective-permute-start | bytes 1671176 | tf_op jit(solution)/shard_map/ppermute | solution.py:284
  73.3 21.1 %collective-permute-start.4 = (f32[8,64,128]{2,1,0:T(8,128)S(1)}, f32[8,64,128]{2,1,0:T(8,128)S(1)}, u32[]{:S(2)}, u32[]{:S(2)}) collective-permute-start(f32[8,64,128]{2,1,0:T(8,128)S(1)} %get-tuple-element.26.s4b), channel_id=1, source_target_pairs={{0,1},{1,2},{2,3},{3,4},{4,5},{5,6},{6,7},{7,8},{8,9},{9,10},{10,1... | collective-permute-start | bytes 786440 | tf_op jit(solution)/shard_map/ppermute | solution.py:284
  75.5 18.9 %collective-permute-start.5 = (f32[8,64,128]{2,1,0:T(8,128)S(1)}, f32[8,64,128]{2,1,0:T(8,128)S(1)}, u32[]{:S(2)}, u32[]{:S(2)}) collective-permute-start(f32[8,64,128]{2,1,0:T(8,128)S(1)} %get-tuple-element.27.s4a), channel_id=1, source_target_pairs={{1,0},{2,1},{3,2},{4,3},{5,4},{6,5},{7,6},{8,7},{9,8},{10,9},{11,1... | collective-permute-start | bytes 786440 | tf_op jit(solution)/shard_map/ppermute | solution.py:284
  81.3 20.4 %all-to-all-start.2 = ((f32[16,4,128]{2,1,0:T(4,128)}), f32[16,4,128]{2,1,0:T(4,128)S(1)}, u32[]{:S(2)}, u32[]{:S(2)}) async-start(f32[16,4,128]{2,1,0:T(4,128)} %broadcast_in_dim.50), calls=%async_computation.2 | async-start | bytes 65536 | tf_op jit(solution)/shard_map/all_to_all | solution.py:289
